TPU v7x, 512 devices: a whole 4x8x8 slice. The times are simulated.
512 devices in a mesh: seq: 64 (over y, z), chan: 8 (over x, core).
Axes of the slice: x: 4, y: 8, z: 8, core: 2. Of those that a mesh axis runs over, the one named last changes fastest.
Arguments:
- query_rows: bfloat16 [24576, 8192], P('seq', 'chan'), may hold values from -6 to 6
- key_rows: bfloat16 [24576, 8192], P('seq', 'chan'), may hold values from -6 to 6
- value_rows: bfloat16 [24576, 8192], P('seq', 'chan'), may hold values from -6 to 6
- residues: float32 [512, 16], P('chan'), may hold values from -9.2 to 9.2
- decay_rates: float32 [512, 16], P('chan'), may hold values from 1.9938151e-06 to 0.0334
- medium_taps: float32 [512, 128], P('chan'), may hold values from -0.5 to 0.5
- out_gain: float32 [8192], P('chan'), may hold values from 0.1 to 1.9
- reader_plan: int32 [512, 9], P('chan'), may hold values from 0 to 63, as said below
Outputs:
- mixed: bfloat16 [24576, 8192], P('seq', 'chan')
- handoff: float32 [640, 16, 128], P('seq', None, 'chan')
Inputs may be any that keep to these rules, and one draw needn't show every extreme that they name: `reader_plan`: each row names 9 different readers. Within each aligned block of 64 filters (the rows of one device along chan) every reader appears at least once, none more than 10 times, and one reader exactly 10 times.
All inputs are finite; a program needn't handle non-finite values.
Results may differ from a plain program's by a relative error of at most 0.0049.
Values may be sent and summed in bfloat16 or wider, within the bound.
A program may use at most 128 MiB of HBM per device.

v0:
```python
import jax
import jax.numpy as jnp
from jax import lax
from jax.sharding import PartitionSpec as P

D = 8192


highest = lax.Precision.HIGHEST


def passed_along(array, axis, by):
    devices = lax.axis_size(axis)
    pairs = [(i, i + by) for i in range(devices) if 0 <= i + by < devices]
    return lax.ppermute(array, axis, pairs)


def entering(part, axis, combine, identity):
    place = lax.axis_index(axis)
    gathered = jax.tree.map(lambda a: lax.all_gather(a, axis), part)
    state = jax.tree.map(lambda a, e: jnp.zeros_like(a) + jnp.asarray(e, a.dtype), part, identity)

    def one(hop, state):
        return combine(
            state, jax.tree.map(lambda a: lax.dynamic_index_in_dim(a, hop, 0, False), gathered)
        )

    return lax.fori_loop(0, place, one, state)


def as_sent(array):
    return jax.tree.map(lambda a: a.astype(jnp.bfloat16) if a.dtype == jnp.float32 else a, array)


def spread(block, axis, holder):
    block = jnp.where(lax.axis_index(axis) == holder, block, jnp.zeros_like(block))
    return lax.psum(block, axis)


def toeplitz_cols(vector):
    size = vector.shape[0] // 2
    tiled = jnp.tile(vector, size)[: size * (2 * size - 1)]
    return tiled.reshape(size, 2 * size - 1)[:, :size]


def per_device(
    query_rows, key_rows, value_rows, residues, decay_rates, medium_taps, out_gain, reader_plan
):
    tokens, channels = query_rows.shape
    groups, mode_count = residues.shape
    group_width = channels // groups
    tail_len = medium_taps.shape[1]
    blocks = tail_len // mode_count
    seq_count = lax.axis_size("seq")
    my_index = lax.axis_index("seq")
    product = (key_rows.astype(jnp.float32) * value_rows.astype(jnp.float32)).astype(jnp.bfloat16)
    norm_factor = jnp.sqrt(-jnp.expm1(-2.0 * decay_rates))
    weighted = residues * norm_factor
    positions = jnp.arange(tokens).astype(jnp.float32)
    grouped = product.reshape(tokens, groups, group_width).transpose(1, 0, 2)
    tail_prev = passed_along(product[tokens - tail_len :], "seq", 1)
    prev_grouped = tail_prev.reshape(tail_len, groups, group_width).transpose(1, 0, 2)

    def per_filter(operands):
        rows, rates, coeffs, taps, prev_rows = operands
        rows = rows.astype(jnp.float32)
        decays = jnp.exp(-rates[:, None] * positions[None, :])
        response = jnp.dot(coeffs, decays, precision=highest) + jnp.pad(
            taps, (0, tokens - tail_len)
        )
        lower = toeplitz_cols(jnp.concatenate([response, jnp.zeros_like(response)]))
        local = lax.dot_general(lower, rows, (((0,), (0,)), ((), ())), precision=highest)
        edge = jnp.concatenate([jnp.zeros((1,), jnp.float32), taps[:0:-1], jnp.zeros_like(taps)])
        carried = jnp.dot(toeplitz_cols(edge), prev_rows.astype(jnp.float32), precision=highest)
        local = local.at[:tail_len].add(carried)
        ends = jnp.exp(-rates[:, None] * (tokens - positions)[None, :])
        own_state = jnp.dot(ends, rows, precision=highest)
        return (local, own_state)

    local, own = lax.map(per_filter, (grouped, decay_rates, weighted, medium_taps, prev_grouped))
    block_decay = jnp.exp(-decay_rates * tokens)[:, :, None]

    def combine(earlier, later):
        return (earlier[0] * later[0], later[0] * earlier[1] + later[1])

    passed, incoming = entering(
        (block_decay, own), "seq", combine, (jnp.ones_like(block_decay), jnp.zeros_like(own))
    )
    starts = jnp.exp(-decay_rates[:, :, None] * positions[None, None, :]) * weighted[:, :, None]
    cross = jnp.einsum("gmt,gmc->tgc", starts, incoming, precision=highest)
    conv = (local.transpose(1, 0, 2) + cross).reshape(tokens, channels)
    gated = query_rows.astype(jnp.float32) * conv
    energy = lax.psum(jnp.sum(gated * gated, axis=1), "chan")
    scale = lax.rsqrt(energy / D + 1e-05)
    mixed = (gated * scale[:, None] * out_gain[None, :]).astype(jnp.bfloat16)
    capacity = (groups * (blocks + 1) + seq_count - 1) // seq_count + 1
    tail_items = (
        product[tokens - tail_len :]
        .astype(jnp.float32)
        .reshape(blocks, mode_count, groups, group_width)
        .transpose(2, 0, 1, 3)
    )
    flat_plan = reader_plan.reshape(-1)
    slots = jnp.arange(capacity)
    item_count = groups * (blocks + 1)
    final = norm_factor[:, :, None] * (block_decay * incoming + own)
    payload = jnp.concatenate([tail_items, final[:, None]], axis=1).reshape(
        item_count, mode_count * group_width
    )
    payload = spread(as_sent(payload), "seq", seq_count - 1).astype(payload.dtype)
    chosen = flat_plan[None, :] == jnp.reshape(my_index, (1,))[:, None]
    ranks = jnp.cumsum(chosen.astype(jnp.int32), axis=1) - 1
    picked = jnp.dot(
        (chosen[:, None, :] & (ranks[:, None, :] == slots[None, :, None])).astype(jnp.float32)[0],
        payload,
        precision=highest,
    )
    handoff = picked.reshape(capacity, mode_count, group_width)
    return (mixed, handoff)


def solution(mesh):
    placed = (
        P("seq", "chan"),
        P("seq", "chan"),
        P("seq", "chan"),
        P("chan", None),
        P("chan", None),
        P("chan", None),
        P("chan"),
        P("chan", None),
    )
    return jax.shard_map(
        per_device,
        mesh=mesh,
        in_specs=placed,
        out_specs=(P("seq", "chan"), P("seq", None, "chan")),
        check_vma=False,
    )
```

profile of v0, /device:TPU:1, one launch (start us, length us, event | category | flops | bytes accessed | tf_op | source)
XLA Modules:
  0.0 919.7 jit_solution(10213384724482302658)
XLA Ops:
  7.2 1.7 multiply_convert_fusion.1
  8.9 4.8 collective-permute-start
  14.4 2.7 collective-permute-done
  17.9 405.4 %while.30 = (s32[]{:T(128)}, f32[64,384,16]{1,2,0:T(8,128)}, f32[64,16,16]{2,1,0:T(8,128)}, f32[64,16]{1,0:T(8,128)S(1)}, f32[64,16]{1,0:T(8,128)S(1)}, /*index=...) while((s32[]{:T(128)}, f32[64,384,16]{1,2,0:T(8,128)}, ...), condition=%wide.region_1.2_spmd.clone.clone, body=%wide.region_0.1_spmd.clone.clone.sunk | while | flops 32727056 | bytes 7412473 | solution.py:80
  19.0 1.2 reshape.237
  25.4 1.2 reshape.237
  31.7 1.2 reshape.237
  38.0 1.2 reshape.237
  44.4 1.2 reshape.237
  50.7 1.2 reshape.237
  57.0 1.2 reshape.237
  423.4 1.7 reshape.217
  425.7 1.5 copy.58
  427.9 51.9 %all-gather.2 = f32[64,64,16]{1,2,0:T(8,128)S(1)} all-gather(f32[1,64,16]{1,2,0:T(8,128)S(1)} %get-tuple-element.294), channel_id=2, replica_groups=mesh['seq'=64,'chan'=8] {'seq'}, dimensions={0}, use_global_device_ids=true | all-gather | bytes 266240 | tf_op jit(solution)/shard_map/all_gather | solution.py:20
  480.1 173.7 %all-gather.5.cloned.1.call-done = f32[4096,16,16]{2,1,0:T(8,128)} async-done(((f32[64,16,16]{2,1,0:T(8,128)}), f32[4096,16,16]{2,1,0:T(8,128)}) %all-gather.5.cloned.1.call-update) | async-done | bytes 4194320 | tf_op jit(solution)/shard_map/all_gather | solution.py:20
  653.8 22.6 %copy.50 = f32[64,64,16,16]{1,3,2,0:T(8,128)} copy(f32[64,64,16,16]{3,2,1,0:T(8,128)} %bitcast.110) | data formatting | bytes 8388608 | tf_op jit(solution)/shard_map/while | solution.py:28
  676.7 1.7 fusion.29
  678.4 1.6 bitcast_add_fusion.1
  680.5 1.5 multiply_reduce_fusion
  682.0 12.8 %psum.14 = f32[384]{0:T(512)S(1)} all-reduce(f32[384]{0:T(512)S(1)} %multiply_reduce_fusion), channel_id=1, replica_groups=mesh['seq'=64,'chan'=8] {'chan'}, use_global_device_ids=true, to_apply=%region_5.6 | all-reduce | flops 384 | bytes 3072 | tf_op jit(solution)/shard_map/psum | solution.py:93
  695.0 2.2 copy.59
  697.2 3.6 select_n.20
  702.8 207.9 %all-reduce.5.cloned.1.call-done = bf16[16,16,576]{2,1,0:T(8,128)(2,1)} async-done(((bf16[16,16,576]{2,1,0:T(8,128)(2,1)}), bf16[16,16,576]{2,1,0:T(8,128)(2,1)}) %all-reduce.5.cloned.1.call-update) | async-done | bytes 294928 | tf_op jit(solution)/shard_map/psum | solution.py:37
  910.7 1.5 fusion.39
  (1518 shorter events, 400.6 us)
Async XLA Ops:
  7.2 646.6 %all-gather.5.cloned.1.call-start = ((), (), s32[]{:S(2)}) async-start(), calls=%async_computation.1 | async-start | bytes 34078720 | tf_op jit(solution)/shard_map/all_gather | solution.py:20
  8.9 5.3 copy-start.3
  8.9 5.4 copy-start.4
  8.9 8.1 collective-permute-start
  423.3 1.8 copy-start.5
  423.3 487.4 %all-reduce.5.cloned.1.call-start = ((), (), s32[]{:S(2)}) async-start(), calls=%async_computation | async-start | bytes 655360 | tf_op jit(solution)/shard_map/psum | solution.py:37
  425.7 54.2 %copy-start.2 = (f32[64,16,16]{2,1,0:T(8,128)S(1)}, f32[64,16,16]{2,1,0:T(8,128)}, u32[]{:S(2)}) copy-start(f32[64,16,16]{2,1,0:T(8,128)} %get-tuple-element.178) | copy-start | bytes 196612
  680.5 14.3 %copy-start.1 = (bf16[64,8,16,16]{0,3,2,1:T(8,128)(2,1)S(1)}, bf16[64,8,16,16]{0,3,2,1:T(8,128)(2,1)}, u32[]{:S(2)}) copy-start(bf16[64,8,16,16]{0,3,2,1:T(8,128)(2,1)} %copy.58) | copy-start | bytes 786436
  697.2 4.5 copy-start
  697.2 4.5 copy-start.6
Sparse Core Ops, SparseCore 0:
  423.4 230.3 all-gather.4
  701.8 208.8 all-reduce.4
where the time goes:
time: 931 us; the launch traced here: 920 us
  waiting for transfers between devices  384 us (41%)
  local copies, waits for them, and re-layouts  293 us (31%)
  matrix products  143 us (15%)
  blocking collectives  64.7 us (7%)
  between operations  14.3 us (2%)
  other arithmetic  13 us (1%)
    psum x1, waiting for transfers between devices, spread(): return lax.psum(block, axis)  208 us
    all_gather x1, waiting for transfers between devices, entering(): gathered = jax.tree.map(lambda a: lax.all_gather(a, axis), part)  174 us
    reshape x128, local copies, waits for them, and re-layouts, toeplitz_cols(): return tiled.reshape(size, 2 * size - 1)[:, :size]  97 us
    dot_general x64, matrix products, per_filter(): jnp.dot(toeplitz_cols(edge), prev_rows.astype(jnp.float32), precision=hig...  52 us
    all_gather x1, blocking collectives, entering(): gathered = jax.tree.map(lambda a: lax.all_gather(a, axis), part)  51.9 us
    dot_general x64, matrix products, per_filter(): own_state = jnp.dot(ends, rows, precision=highest)  51.6 us
    dynamic_slice x64, local copies, waits for them, and re-layouts, per_device(): lax.map(per_filter, (grouped, decay_rates, weighted, medium_taps, prev_gr...  44.7 us
    squeeze x64, local copies, waits for them, and re-layouts, per_device(): lax.map(per_filter, (grouped, decay_rates, weighted, medium_taps, prev_gr...  44.7 us
  transfers between devices with their start and end apart: 3, of which 3 were waited for; matrix products, arithmetic and copies ran while one was open for 1% of the time, Pallas kernels for 0%

commit v1 on v0

v1 whole, which is shorter than its diff:
```python
import functools
import math

import jax
import jax.numpy as jnp
from jax import lax
from jax.experimental import pallas as pl
from jax.experimental.pallas import tpu as pltpu
from jax.sharding import PartitionSpec as P

D = 8192
GW = 16
MODES = 16
MED = 128
NB = 8
SLOTS = 16
LANES = 128
F32 = jnp.float32
BF16 = jnp.bfloat16
MESH = pl.DeviceIdType.MESH


def iota(shape, axis):
    return lax.broadcasted_iota(jnp.int32, shape, axis)


def split(x, parts):
    out = []
    for _ in range(parts):
        piece = x.astype(BF16)
        out.append(piece)
        x = x - piece.astype(F32)
    return out


def one_minus_exp_neg(x):
    small = x * (1.0 - x * (1 / 2) * (1.0 - x * (1 / 3) * (1.0 - x * (1 / 4) * (
        1.0 - x * (1 / 5) * (1.0 - x * (1 / 6) * (1.0 - x * (1 / 7)))))))
    return jnp.where(x < 0.1, small, 1.0 - jnp.exp(-x))


def dot(a, b):
    return jnp.dot(a, b, preferred_element_type=F32)


def swap_blocks(x):
    n = x.shape[0]
    sub = iota((n, 8, LANES), 1)
    blk = iota((n, 8, LANES), 2) // GW
    gap = (blk - sub + 8) % 8
    out = x
    for d in range(1, 8):
        moved = pltpu.roll(pltpu.roll(x, 8 - d, 1), GW * d, 2)
        out = jnp.where(gap == d, moved, out)
    return out


def kernel(cfg, q_hbm, k_hbm, v_hbm, res_ref, lam_ref, taps_ref, gain_ref, plan_ref,
           out_hbm, hand_ref,
           kbuf, vbuf, qbuf, xbuf, hbuf, lamc, wc, eb, lame, gh, gt, tmat, smat, rhs, local, st,
           a1s, a1r, pre, a2s, a2r, a3s, a3r, items, pk, row, tin, es, er, obuf,
           in_sem, out_sem, s1, r1, s2, r2, s3, r3, sx, rx, sh, rh, sp, rp, sf, rf):
    ny, nz, nc, tiles, tokens = cfg
    groups = tiles * 8
    chunks = tokens // MED
    me = lax.axis_index("seq")
    ch = lax.axis_index("chan")
    y = me // nz
    z = me % nz
    last = ny * nz - 1

    for c in range(chunks):
        rows = pl.ds(c * MED, MED)
        pltpu.make_async_copy(k_hbm.at[rows], kbuf.at[rows], in_sem.at[0, c]).start()
        pltpu.make_async_copy(v_hbm.at[rows], vbuf.at[rows], in_sem.at[1, c]).start()
    pltpu.make_async_copy(q_hbm, qbuf, in_sem.at[2, 0]).start()

    barrier = pltpu.get_barrier_semaphore()

    def greet(seq, chan):
        pl.semaphore_signal(barrier, inc=1, device_id=(seq, chan), device_id_type=MESH)

    for d in range(1, nz):
        greet(y * nz + (z + d) % nz, ch)
    for d in range(1, ny):
        greet(((y + d) % ny) * nz + z, ch)
    for d in range(1, nc):
        greet(me, (ch + d) % nc)
    wraps_on = (z == nz - 1) & (y < ny - 1)
    wraps_in = (z == 0) & (y > 0)

    @pl.when(wraps_on)
    def _():
        greet(me + 1, ch)

    @pl.when(wraps_in)
    def _():
        greet(me - 1, ch)

    lam_t = jnp.transpose(lam_ref[...])
    res_t = jnp.transpose(res_ref[...])
    lane16 = iota((MODES, LANES), 1) // GW
    lane128 = iota((LANES, LANES), 1)
    back = (LANES - lane128).astype(F32)
    for g in range(tiles):
        spread = jnp.zeros((MODES, LANES), F32)
        cols = []
        rescols = []
        for k in range(8):
            f = g * 8 + k
            col = jnp.broadcast_to(lam_t[:, f:f + 1], (MODES, LANES))
            cols.append(col)
            rescols.append(jnp.broadcast_to(res_t[:, f:f + 1], (MODES, LANES)))
            spread = jnp.where(lane16 == k, col, spread)
        lame[:, g * LANES:(g + 1) * LANES] = spread
        rates = jnp.concatenate(cols, axis=0)
        lamc[g * LANES:(g + 1) * LANES, :] = rates
        weight = jnp.concatenate(rescols, axis=0) * jnp.sqrt(one_minus_exp_neg(2.0 * rates))
        wc[g * LANES:(g + 1) * LANES, :] = weight
        e = jnp.exp(-rates * back)
        hi, lo = split(e, 2)
        eb[g, 0:LANES, :] = hi
        eb[g, LANES:2 * LANES, :] = lo
        modal = jnp.where(lane128 == 0, weight, weight * e)
        gh[g * 8:(g + 1) * 8, :] = jnp.sum(modal.reshape(8, MODES, LANES), axis=1)

    for c in range(chunks):
        rows = pl.ds(c * MED, MED)
        pltpu.make_async_copy(k_hbm.at[rows], kbuf.at[rows], in_sem.at[0, c]).wait()
        pltpu.make_async_copy(v_hbm.at[rows], vbuf.at[rows], in_sem.at[1, c]).wait()
        xbuf[rows, :] = (kbuf[rows, :].astype(F32) * vbuf[rows, :].astype(F32)).astype(BF16)

    own16 = iota((MODES, LANES), 1) // GW
    for g in range(tiles):
        lanes = slice(g * LANES, (g + 1) * LANES)
        total = None
        d128 = jnp.exp(lame[:, lanes] * (-float(MED)))
        both = [xbuf[c * MED:(c + 1) * MED, lanes] for c in range(chunks)]
        raw = dot(eb[g], jnp.concatenate(both, axis=1))
        raw = raw[0:LANES] + raw[LANES:2 * LANES]
        for c in range(chunks):
            part = jnp.zeros((MODES, LANES), F32)
            for k in range(8):
                piece = raw[k * MODES:(k + 1) * MODES, c * LANES:(c + 1) * LANES]
                part = jnp.where(own16 == k, piece, part)
            total = part if total is None else total * d128 + part
            if c < chunks - 1:
                st[c, :, lanes] = total
        a1s[g] = total.astype(BF16)

    extra = wraps_on.astype(jnp.int32) + wraps_in.astype(jnp.int32)
    pl.semaphore_wait(barrier, (nz - 1) + (ny - 1) + (nc - 1) + extra)

    def remote(src, dst, send, recv, seq, chan):
        return pltpu.make_async_remote_copy(
            src_ref=src, dst_ref=dst, send_sem=send, recv_sem=recv,
            device_id=(seq, chan), device_id_type=MESH)

    def order(n):
        return sorted(range(1, n), key=lambda d: -min(d, n - d))

    sent1 = []
    for d in order(nz):
        to = (z + d) % nz
        copy = remote(a1s.at[to], a1r.at[z], s1.at[d], r1.at[z], y * nz + to, ch)
        copy.start()
        sent1.append(copy)
    a1r[z] = a1s[z]

    def halo():
        return remote(xbuf.at[pl.ds(tokens - MED, MED)], hbuf, sh, rh, me + 1, ch)

    @pl.when(me < last)
    def _():
        halo().start()

    plan = plan_ref[...]
    tri = (iota((groups, groups), 1) < iota((groups, groups), 0)).astype(BF16)

    @pl.when(me == last)
    def _():
        who = iota((groups, LANES), 1)
        hits = jnp.zeros((groups, LANES), F32)
        for b in range(NB + 1):
            hits = hits + (plan[:, b:b + 1] == who).astype(F32)
        before = dot(tri, hits.astype(BF16))
        slots = jnp.full((groups, LANES), -1.0, F32)
        for b in range(NB):
            reader = plan[:, b:b + 1]
            rank = jnp.sum(jnp.where(reader == who, before, 0.0), axis=1, keepdims=True)
            slot = reader.astype(F32) * SLOTS + rank
            slots = jnp.where(who == b, slot, slots)
        slots_t = jnp.transpose(slots)
        for b in range(NB):
            for half in range(2):
                first = tokens - MED + b * MODES + half * 8
                for g in range(tiles):
                    tile = xbuf[tokens - MED + b * MODES:tokens - MED + (b + 1) * MODES,
                                g * LANES:(g + 1) * LANES].astype(F32)[half * 8:half * 8 + 8]
                    items[b * groups + g * 8:b * groups + g * 8 + 8,
                          half * LANES:(half + 1) * LANES] = swap_blocks(tile[None])[0]
        for part in range(ny):
            count = nz * SLOTS
            base = part * count
            acc = jnp.zeros((count, 2 * LANES), F32)
            for b in range(NB):
                target = (iota((count, groups), 0) + base).astype(F32)
                pick = (target == slots_t[b:b + 1, 0:groups]).astype(BF16)
                acc = acc + dot(pick, items[b * groups:(b + 1) * groups, :].astype(BF16))
            packed = acc.astype(BF16).reshape(nz, SLOTS, 2 * LANES)
            if part == ny - 1:
                row[...] = packed
            else:
                pk[part] = packed

    def pack_copy(part):
        return remote(pk.at[part], row, sp.at[part], rp, part * nz + nz - 1, ch)

    @pl.when(me == last)
    def _():
        for part in range(ny - 1):
            pack_copy(part).start()

    perm = (iota((LANES, LANES), 0) == (LANES - iota((LANES, LANES), 1)) % LANES).astype(BF16)
    flipped = dot(jnp.concatenate(split(taps_ref[...], 3), axis=0), perm)
    flipped = flipped[0:groups] + flipped[groups:2 * groups] + flipped[2 * groups:3 * groups]
    gt[...] = flipped
    gh[...] = gh[...] + flipped

    def conv_tile(g, carry):
        lanes = pl.ds(pl.multiple_of(g * LANES, LANES), LANES)
        rows8 = pl.ds(pl.multiple_of(g * 8, 8), 8)
        full = gh[rows8, :]
        taps = gt[rows8, :]
        lower = iota((LANES, LANES), 1) <= iota((LANES, LANES), 0)
        which = iota((MED, LANES), 1) // GW
        x0 = xbuf[0:MED, lanes]
        x1 = xbuf[MED:2 * MED, lanes]
        x2 = xbuf[2 * MED:3 * MED, lanes]
        for k in range(8):
            a = pltpu.roll(jnp.broadcast_to(full[k:k + 1], (LANES, LANES)), 0, 1, stride=1, stride_axis=0)
            b = pltpu.roll(jnp.broadcast_to(taps[k:k + 1], (LANES, LANES)), 0, 1, stride=1, stride_axis=0)
            cols = slice(k * LANES, (k + 1) * LANES)
            tmat[g, 0:LANES, cols] = jnp.where(lower, a, 0.0).astype(BF16)
            tmat[g, LANES:2 * LANES, cols] = jnp.where(lower, 0.0, b).astype(BF16)
            keep = (which == k).astype(BF16)
            rhs[cols, 0:LANES] = x0 * keep
            rhs[cols, LANES:2 * LANES] = x1 * keep
            rhs[cols, 2 * LANES:3 * LANES] = x2 * keep
        out = dot(tmat[g], rhs[:, 0:2 * LANES])
        out2 = dot(tmat[g, 0:LANES, :], rhs[:, 2 * LANES:3 * LANES])
        local[0:MED, lanes] = out[0:LANES, 0:LANES]
        local[MED:2 * MED, lanes] = out[0:LANES, LANES:2 * LANES] + out[LANES:2 * LANES, 0:LANES]
        local[2 * MED:3 * MED, lanes] = out2 + out[LANES:2 * LANES, LANES:2 * LANES]
        return carry

    lax.fori_loop(0, tiles, conv_tile, 0)

    mine = pl.ds(pl.multiple_of(z * LANES, LANES), LANES)
    lam_s = lame[:, mine]
    d_dev = jnp.exp(lam_s * (-float(tokens)))
    for d in range(1, nz):
        frm = (z - d + nz) % nz
        remote(a1s.at[0], a1r.at[frm], s1.at[d], r1.at[frm], me, ch).wait_recv()
    run = jnp.zeros((MODES, LANES), F32)
    for i in range(nz):
        pre[i] = run
        run = run * d_dev + a1r[i].astype(F32)
    a2s[...] = run.astype(BF16)

    sent2 = []
    for d in order(ny):
        to = (y + d) % ny
        copy = remote(a2s, a2r.at[y], s2.at[d], r2.at[y], to * nz + z, ch)
        copy.start()
        sent2.append(copy)
    a2r[y] = a2s[...]

    def carry_tile(g, carry):
        lanes = pl.ds(pl.multiple_of(g * LANES, LANES), LANES)
        rates = lamc[lanes, :]
        weight = wc[lanes, :]
        at = lane128.astype(F32)
        for c in range(chunks):
            s = weight * jnp.exp(-rates * (at + float(c * MED)))
            smat[c * MED:(c + 1) * MED, lanes] = jnp.transpose(s).astype(BF16)
        same = (iota((LANES, LANES), 0) // MODES) == (iota((LANES, LANES), 1) // GW)
        pieces = []
        for c in range(chunks - 1):
            state = jnp.concatenate([st[c, :, lanes]] * 8, axis=0)
            pieces.append(jnp.where(same, state, 0.0))
        hi, lo = split(jnp.concatenate(pieces, axis=1), 2)
        factor = smat[0:MED, lanes]
        out = dot(factor, hi) + dot(factor, lo)
        for c in range(chunks - 1):
            rows = slice((c + 1) * MED, (c + 2) * MED)
            local[rows, lanes] = local[rows, lanes] + out[:, c * LANES:(c + 1) * LANES]
        return carry

    lax.fori_loop(0, tiles, carry_tile, 0)

    d_row = jnp.exp(lam_s * (-float(tokens * nz)))
    for d in range(1, ny):
        frm = (y - d + ny) % ny
        remote(a2s, a2r.at[frm], s2.at[d], r2.at[frm], me, ch).wait_recv()
    run = jnp.zeros((MODES, LANES), F32)
    above = jnp.zeros((MODES, LANES), F32)
    for i in range(ny):
        above = jnp.where(y == i, run, above)
        run = run * d_row + a2r[i].astype(F32)
    norm_s = jnp.sqrt(one_minus_exp_neg(2.0 * lam_s))
    final = (run * norm_s).astype(BF16)
    for i in range(nz):
        a3s[i, 0] = (above + pre[i]).astype(BF16)
        a3s[i, 1] = final
        above = above * d_dev

    sent3 = []
    for d in order(nz):
        to = (z + d) % nz
        copy = remote(a3s.at[to], a3r.at[z], s3.at[d], r3.at[z], y * nz + to, ch)
        copy.start()
        sent3.append(copy)
    a3r[z] = a3s[z]

    def hop_copy(to):
        return remote(row.at[to], tin, sf.at[to], rf, y * nz + to, ch)

    @pl.when((z == nz - 1) & (me != last))
    def _():
        remote(pk.at[0], row, sp.at[0], rp, me, ch).wait_recv()

    @pl.when(z == nz - 1)
    def _():
        for to in range(nz - 1):
            hop_copy(to).start()
        tin[...] = row[nz - 1]

    @pl.when(me > 0)
    def _():
        remote(xbuf.at[pl.ds(tokens - MED, MED)], hbuf, sh, rh, me, ch).wait_recv()

        def halo_tile(g, carry):
            lanes = pl.ds(pl.multiple_of(g * LANES, LANES), LANES)
            which = iota((MED, LANES), 1) // GW
            xh = hbuf[:, lanes]
            for k in range(8):
                rhs[k * LANES:(k + 1) * LANES, 0:LANES] = xh * (which == k).astype(BF16)
            out = dot(tmat[g, LANES:2 * LANES, :], rhs[:, 0:LANES])
            local[0:MED, lanes] = local[0:MED, lanes] + out
            return carry

        lax.fori_loop(0, tiles, halo_tile, 0)

    pltpu.make_async_copy(q_hbm, qbuf, in_sem.at[2, 0]).wait()
    for d in range(1, nz):
        frm = (z - d + nz) % nz
        remote(a3s.at[0], a3r.at[frm], s3.at[d], r3.at[frm], me, ch).wait_recv()

    power = jnp.zeros((tokens, LANES), F32)
    wide = 2 * LANES
    same2 = ((iota((wide, wide), 0) // MODES) == (iota((wide, wide), 1) // GW)).astype(BF16)
    for g in range(tiles // 2):
        lanes = slice(g * wide, (g + 1) * wide)
        state = jnp.concatenate([a3r[2 * g, 0], a3r[2 * g + 1, 0]], axis=1)
        spread = jnp.concatenate([state] * 16, axis=0) * same2
        cross = dot(smat[:, lanes], spread)
        gated = qbuf[:, lanes].astype(F32) * (local[:, lanes] + cross)
        local[:, lanes] = gated
        sq = gated * gated
        power = power + sq[:, 0:LANES] + sq[:, LANES:wide]
    es[...] = jnp.sum(jnp.transpose(power), axis=0, keepdims=True)

    sentx = []
    for d in order(nc):
        to = (ch + d) % nc
        copy = remote(es, er.at[ch], sx.at[d], rx.at[ch], me, to)
        copy.start()
        sentx.append(copy)
    er[ch] = es[...]

    mine_hit = (plan == me)
    hit = jnp.sum(mine_hit.astype(F32), axis=1, keepdims=True)
    before = dot(tri, jnp.broadcast_to(hit, (groups, 2 * LANES)).astype(BF16))
    slot = (iota((groups, 2 * LANES), 1) // GW).astype(F32)
    wants = ((before == slot) & mine_hit[:, NB:NB + 1]).astype(BF16)
    picked = jnp.zeros((MODES, 2 * LANES), F32)
    delta = ((iota((LANES, 2 * LANES), 0) % GW) == (iota((LANES, 2 * LANES), 1) % GW)).astype(F32)
    for g in range(tiles):
        rep = ((iota((LANES, groups), 0) // GW + g * 8) == iota((LANES, groups), 1)).astype(BF16)
        choose = (dot(rep, wants) * delta).astype(BF16)
        picked = picked + dot(a3r[g, 1], choose)

    @pl.when(z != nz - 1)
    def _():
        remote(row.at[0], tin, sf.at[0], rf, me, ch).wait_recv()

    tails = tin[...].astype(F32)
    for a in range(2):
        for b in range(2):
            block = swap_blocks(tails[8 * a:8 * a + 8, b * LANES:(b + 1) * LANES][None])[0]
            block = block + picked[8 * b:8 * b + 8, a * LANES:(a + 1) * LANES]
            for k in range(8):
                j = a * 8 + k
                if j < 10:
                    hand_ref[j, 8 * b:8 * b + 8, :] = block[:, k * GW:(k + 1) * GW]

    for d in range(1, nc):
        frm = (ch - d + nc) % nc
        remote(es, er.at[frm], sx.at[d], rx.at[frm], me, ch).wait_recv()
    energy = er[0]
    for i in range(1, nc):
        energy = energy + er[i]
    scale = lax.rsqrt(energy / (nc * tiles * LANES) + 1e-05)
    scale = jnp.transpose(jnp.broadcast_to(scale, (LANES, tokens)))
    for c in range(chunks):
        rows = slice(c * MED, (c + 1) * MED)
        for g in range(tiles):
            lanes = slice(g * LANES, (g + 1) * LANES)
            obuf[rows, lanes] = (local[rows, lanes] * scale[rows] * gain_ref[:, lanes]).astype(BF16)
        pltpu.make_async_copy(obuf.at[rows], out_hbm.at[rows], out_sem.at[c]).start()

    for copy in sent1 + sent2 + sent3 + sentx:
        copy.wait_send()

    @pl.when(me < last)
    def _():
        halo().wait_send()

    @pl.when(me == last)
    def _():
        for part in range(ny - 1):
            pack_copy(part).wait_send()

    @pl.when(z == nz - 1)
    def _():
        for to in range(nz - 1):
            hop_copy(to).wait_send()

    for c in range(chunks):
        rows = slice(c * MED, (c + 1) * MED)
        pltpu.make_async_copy(obuf.at[rows], out_hbm.at[rows], out_sem.at[c]).wait()


def per_device(query_rows, key_rows, value_rows, residues, decay_rates, medium_taps, out_gain, reader_plan):
    tokens, channels = query_rows.shape
    tiles = channels // LANES
    groups = tiles * 8
    seq = lax.axis_size("seq")
    nz = math.isqrt(seq)
    ny = seq // nz
    nc = lax.axis_size("chan")
    cfg = (ny, nz, nc, tiles, tokens)
    chunks = tokens // MED
    vm = pltpu.VMEM
    dma = pltpu.SemaphoreType.DMA
    scratch = [
        vm((tokens, channels), BF16), vm((tokens, channels), BF16), vm((tokens, channels), BF16),
        vm((tokens, channels), BF16), vm((MED, channels), BF16),
        vm((channels, LANES), F32), vm((channels, LANES), F32), vm((tiles, 2 * LANES, LANES), BF16),
        vm((MODES, channels), F32), vm((groups, LANES), F32), vm((groups, LANES), F32),
        vm((tiles, 2 * LANES, 8 * LANES), BF16), vm((tokens, channels), BF16),
        vm((8 * LANES, 3 * LANES), BF16), vm((tokens, channels), F32),
        vm((chunks, MODES, channels), F32),
        vm((nz, MODES, LANES), BF16), vm((nz, MODES, LANES), BF16), vm((nz, MODES, LANES), F32),
        vm((MODES, LANES), BF16), vm((ny, MODES, LANES), BF16),
        vm((nz, 2, MODES, LANES), BF16), vm((nz, 2, MODES, LANES), BF16),
        vm((NB * groups, 2 * LANES), F32), vm((ny - 1, nz, SLOTS, 2 * LANES), BF16),
        vm((nz, SLOTS, 2 * LANES), BF16), vm((SLOTS, 2 * LANES), BF16),
        vm((1, tokens), F32), vm((nc, 1, tokens), F32), vm((tokens, channels), BF16),
        dma((3, chunks)), dma((chunks,)),
        dma((nz,)), dma((nz,)), dma((ny,)), dma((ny,)), dma((nz,)), dma((nz,)), dma((nc,)), dma((nc,)),
        dma, dma, dma((ny,)), dma, dma((nz,)), dma,
    ]
    hbm = pl.BlockSpec(memory_space=pl.ANY)
    vmem = pl.BlockSpec(memory_space=pltpu.VMEM)
    return pl.pallas_call(
        functools.partial(kernel, cfg),
        name="hyena",
        out_shape=(
            jax.ShapeDtypeStruct((tokens, channels), BF16),
            jax.ShapeDtypeStruct((10, MODES, GW), F32),
        ),
        in_specs=[hbm, hbm, hbm, vmem, vmem, vmem, vmem, vmem],
        out_specs=(hbm, vmem),
        scratch_shapes=scratch,
        compiler_params=pltpu.CompilerParams(
            collective_id=0, has_side_effects=True, vmem_limit_bytes=48 * 1024 * 1024),
    )(query_rows, key_rows, value_rows, residues, decay_rates, medium_taps,
      out_gain.reshape(1, channels), reader_plan)


def solution(mesh):
    placed = (
        P("seq", "chan"),
        P("seq", "chan"),
        P("seq", "chan"),
        P("chan", None),
        P("chan", None),
        P("chan", None),
        P("chan"),
        P("chan", None),
    )
    return jax.shard_map(
        per_device,
        mesh=mesh,
        in_specs=placed,
        out_specs=(P("seq", "chan"), P("seq", None, "chan")),
        check_vma=False,
    )
```

time: 931 us -> 45.6 us (0.05); the launches traced: 920 us -> 45.2 us
  waiting for transfers between devices: 384 us -> 0 us
  local copies, waits for them, and re-layouts: 293 us -> 7.08 us
  matrix products: 143 us -> 0 us
  blocking collectives: 64.7 us -> 0 us
  Pallas kernels: 0 us -> 37.4 us
  between operations: 14.3 us -> 0.67 us
  other arithmetic: 13 us -> 0 us
    psum x1 -> x0, waiting for transfers between devices: 208 us -> none  [spread(): return lax.psum(block, axis)]
    all_gather x1 -> x0, waiting for transfers between devices: 174 us -> none  [entering(): gathered = jax.tree.map(lambda a: lax.all_gather(a, axis), part)]
    dot_general x258 -> x0, matrix products: 143 us -> none  [the longest x64 52 us: per_filter(): jnp.dot(toeplitz_cols(edge), prev_rows.astype(jnp.float32), precision=hig...]
    reshape x130 -> x0, local copies, waits for them, and re-layouts: 99.1 us -> none  [the longest x128 97 us: toeplitz_cols(): return tiled.reshape(size, 2 * size - 1)[:, :size]]
    all_gather x1 -> x0, blocking collectives: 51.9 us -> none  [entering(): gathered = jax.tree.map(lambda a: lax.all_gather(a, axis), part)]
    dynamic_slice x64 -> x0, local copies, waits for them, and re-layouts: 44.7 us -> none  [per_device(): lax.map(per_filter, (grouped, decay_rates, weighted, medium_taps, prev_gr...]
    squeeze x64 -> x0, local copies, waits for them, and re-layouts: 44.7 us -> none  [per_device(): lax.map(per_filter, (grouped, decay_rates, weighted, medium_taps, prev_gr...]
    dynamic_update_slice x64 -> x0, local copies, waits for them, and re-layouts: 43 us -> none  [per_device(): lax.map(per_filter, (grouped, decay_rates, weighted, medium_taps, prev_gr...]
  transfers between devices with their start and end apart: 3 -> 0, of which waited for: 3 -> 0; matrix products, arithmetic and copies ran while one was open for 1% -> 0% of each run, Pallas kernels for 0% -> 0%
where the time goes in v1:
time: 45.6 us; the launch traced here: 45.2 us
  Pallas kernels  37.4 us (82%)
  local copies, waits for them, and re-layouts  7.08 us (16%)
  between operations  0.67 us (1%)
    pallas_call x1, Pallas kernels, per_device(): pl.pallas_call(functools.partial(kernel, cfg), name='hyena', out_shape=(j...  37.4 us
    unnamed x19, local copies, waits for them, and re-layouts  7.08 us

profile of v1, /device:TPU:1, one launch (start us, length us, event | category | flops | bytes accessed | tf_op | source)
XLA Modules:
  0.0 45.2 jit_solution(3330974035079980514)
XLA Ops:
  0.6 0.0 copy-start.5
  0.6 0.8 %copy.10.res_ref = f32[64,16]{1,0:T(8,128)S(1)} copy(f32[64,16]{0,1:T(8,128)} %param.11) | data formatting | bytes 8192 | tf_op args[3]
  1.4 0.0 copy-done.5
  1.4 0.0 copy-start.6
  1.4 0.0 copy-start.3
  1.4 0.1 copy.11.lam_ref
  1.5 0.6 %copy-done.6 = s32[64,9]{0,1:T(8,128)S(1)} copy-done((s32[64,9]{0,1:T(8,128)S(1)}, s32[64,9]{0,1:T(8,128)}, u32[]{:S(2)}) %copy-start.6) | copy-done | bytes 2328
  2.1 0.0 copy-start.4
  2.1 0.1 copy.12.plan_ref
  2.2 0.0 copy-done.3
  2.2 0.6 %copy-done.4 = f32[1024]{0:T(1024)S(1)} copy-done((f32[1024]{0:T(1024)S(1)}, f32[1024]{0:T(1024)}, u32[]{:S(2)}) %copy-start.4) | copy-done | bytes 4120
  2.8 0.0 copy-start
  2.8 1.1 %copy-done = bf16[384,1024]{1,0:T(8,128)(2,1)S(1)} copy-done((bf16[384,1024]{1,0:T(8,128)(2,1)S(1)}, bf16[384,1024]{1,0:T(8,128)(2,1)}, u32[]{:S(2)}) %copy-start) | copy-done | bytes 786456
  4.0 0.0 copy-start.1
  4.0 1.1 %copy-done.1 = bf16[384,1024]{1,0:T(8,128)(2,1)S(1)} copy-done((bf16[384,1024]{1,0:T(8,128)(2,1)S(1)}, bf16[384,1024]{1,0:T(8,128)(2,1)}, u32[]{:S(2)}) %copy-start.1) | copy-done | bytes 786456
  5.1 0.0 copy-start.2
  5.1 1.1 %copy-done.2 = bf16[384,1024]{1,0:T(8,128)(2,1)S(1)} copy-done((bf16[384,1024]{1,0:T(8,128)(2,1)S(1)}, bf16[384,1024]{1,0:T(8,128)(2,1)}, u32[]{:S(2)}) %copy-start.2) | copy-done | bytes 786456
  6.2 37.4 %hyena.1 = (bf16[384,1024]{1,0:T(8,128)(2,1)S(1)}, f32[10,16,16]{2,1,0:T(8,128)S(1)}) custom-call(bf16[384,1024]{1,0:T(8,128)(2,1)S(1)} %copy-done, bf16[384,1024]{1,0:T(8,128)(2,1)S(1)} %copy-done.1, bf16[384,1024]{1,0:T(8,128)(2,1)S(1)} %copy-done.2, f32[64,16]{1,0:T(8,128)S(1)} %copy.10.res_ref, f32[64,16]{1,0:T(8,128)S(1)} %copy.11.lam_ref, ...), custom_call_target="tpu_custom_call" | custom-call | tf_op jit(solution)/shard_map/hyena/pallas_call | solution.py:477
  43.7 0.9 %copy.15 = bf16[384,1024]{1,0:T(8,128)(2,1)} copy(bf16[384,1024]{1,0:T(8,128)(2,1)S(1)} %get-tuple-element.4) | data formatting | bytes 1572864
  44.5 0.6 %copy.16 = f32[10,16,16]{2,1,0:T(8,128)} copy(f32[10,16,16]{2,1,0:T(8,128)S(1)} %get-tuple-element.5) | data formatting | bytes 20480
Async XLA Ops:
  0.6 0.8 %copy-start.5 = (f32[64,16]{0,1:T(8,128)S(1)}, f32[64,16]{0,1:T(8,128)}, u32[]{:S(2)}) copy-start(f32[64,16]{0,1:T(8,128)} %param.12) | copy-start | bytes 12292
  1.4 0.7 %copy-start.6 = (s32[64,9]{0,1:T(8,128)S(1)}, s32[64,9]{0,1:T(8,128)}, u32[]{:S(2)}) copy-start(s32[64,9]{0,1:T(8,128)} %param.15) | copy-start | bytes 6916
  1.4 0.8 %copy-start.3 = (f32[64,128]{1,0:T(8,128)S(1)}, f32[64,128]{1,0:T(8,128)}, u32[]{:S(2)}) copy-start(f32[64,128]{1,0:T(8,128)} %taps_ref.1) | copy-start | bytes 98308
  2.1 0.7 %copy-start.4 = (f32[1024]{0:T(1024)S(1)}, f32[1024]{0:T(1024)}, u32[]{:S(2)}) copy-start(f32[1024]{0:T(1024)} %param.14) | copy-start | bytes 12292
  2.8 1.1 %copy-start = (bf16[384,1024]{1,0:T(8,128)(2,1)S(1)}, bf16[384,1024]{1,0:T(8,128)(2,1)}, u32[]{:S(2)}) copy-start(bf16[384,1024]{1,0:T(8,128)(2,1)} %q_hbm.1) | copy-start | bytes 2359300
  4.0 1.1 %copy-start.1 = (bf16[384,1024]{1,0:T(8,128)(2,1)S(1)}, bf16[384,1024]{1,0:T(8,128)(2,1)}, u32[]{:S(2)}) copy-start(bf16[384,1024]{1,0:T(8,128)(2,1)} %k_hbm.1) | copy-start | bytes 2359300
  5.1 1.1 %copy-start.2 = (bf16[384,1024]{1,0:T(8,128)(2,1)S(1)}, bf16[384,1024]{1,0:T(8,128)(2,1)}, u32[]{:S(2)}) copy-start(bf16[384,1024]{1,0:T(8,128)(2,1)} %v_hbm.1) | copy-start | bytes 2359300

commit v2 on v1

--- a/solution.py
+++ b/solution.py
@@ -39,6 +39,10 @@
     return jnp.where(x < 0.1, small, 1.0 - jnp.exp(-x))
 
 
+LOG2E = 1.4426950408889634
+LN2 = 0.6931471805599453
+
+
 def dot(a, b):
     return jnp.dot(a, b, preferred_element_type=F32)
 
@@ -55,11 +59,11 @@
     return out
 
 
-def kernel(cfg, q_hbm, k_hbm, v_hbm, res_ref, lam_ref, taps_ref, gain_ref, plan_ref,
-           out_hbm, hand_ref,
-           kbuf, vbuf, qbuf, xbuf, hbuf, lamc, wc, eb, lame, gh, gt, tmat, smat, rhs, local, st,
-           a1s, a1r, pre, a2s, a2r, a3s, a3r, items, pk, row, tin, es, er, obuf,
-           in_sem, out_sem, s1, r1, s2, r2, s3, r3, sx, rx, sh, rh, sp, rp, sf, rf):
+def kernel(cfg, q_hbm, k_hbm, v_hbm, res_hbm, lam_hbm, taps_hbm, plan_hbm,
+           local, hand_ref, energy_ref,
+           kbuf, vbuf, qbuf, xbuf, hbuf, lam_v, res_v, taps_v, plan_v, lamc, eb, lame, gh, gt, tmat, smat, rhs, st,
+           a1s, a1r, pre, a2s, a2r, a3s, a3r, items, pk, row, tin, es, er,
+           in_sem, s1, r1, s2, r2, s3, r3, sx, rx, sh, rh, sp, rp, sf, rf):
     ny, nz, nc, tiles, tokens = cfg
     groups = tiles * 8
     chunks = tokens // MED
@@ -69,11 +73,26 @@
     z = me % nz
     last = ny * nz - 1
 
+    def fetch(src, dst, a, b):
+        return pltpu.make_async_copy(src, dst, in_sem.at[a, b])
+
+    def fetch_rows(c):
+        rows = pl.ds(c * MED, MED)
+        return (fetch(k_hbm.at[rows], kbuf.at[rows], 0, c), fetch(v_hbm.at[rows], vbuf.at[rows], 1, c))
+
+    get_lam = fetch(lam_hbm, lam_v, 2, 0)
+    get_res = fetch(res_hbm, res_v, 2, 1)
+    get_taps = fetch(taps_hbm, taps_v, 2, 2)
+    get_plan = fetch(plan_hbm, plan_v, 3, 0)
+    get_q = fetch(q_hbm, qbuf, 3, 1)
+    get_lam.start()
     for c in range(chunks):
-        rows = pl.ds(c * MED, MED)
-        pltpu.make_async_copy(k_hbm.at[rows], kbuf.at[rows], in_sem.at[0, c]).start()
-        pltpu.make_async_copy(v_hbm.at[rows], vbuf.at[rows], in_sem.at[1, c]).start()
-    pltpu.make_async_copy(q_hbm, qbuf, in_sem.at[2, 0]).start()
+        for copy in fetch_rows(c):
+            copy.start()
+    get_res.start()
+    get_taps.start()
+    get_plan.start()
+    get_q.start()
 
     barrier = pltpu.get_barrier_semaphore()
 
@@ -97,47 +116,36 @@
     def _():
         greet(me - 1, ch)
 
-    lam_t = jnp.transpose(lam_ref[...])
-    res_t = jnp.transpose(res_ref[...])
-    lane16 = iota((MODES, LANES), 1) // GW
+    get_lam.wait()
+    lam_t = lam_v[...]
+    lam2 = lam_t * LOG2E
+    own16 = iota((MODES, LANES), 1) // GW
     lane128 = iota((LANES, LANES), 1)
-    back = (LANES - lane128).astype(F32)
+    back = (iota((MODES, LANES), 1) - LANES).astype(F32)
     for g in range(tiles):
         spread = jnp.zeros((MODES, LANES), F32)
-        cols = []
-        rescols = []
         for k in range(8):
             f = g * 8 + k
-            col = jnp.broadcast_to(lam_t[:, f:f + 1], (MODES, LANES))
-            cols.append(col)
-            rescols.append(jnp.broadcast_to(res_t[:, f:f + 1], (MODES, LANES)))
-            spread = jnp.where(lane16 == k, col, spread)
+            col = jnp.broadcast_to(lam2[:, f:f + 1], (MODES, LANES))
+            spread = jnp.where(own16 == k, col, spread)
+            lamc[f * MODES:(f + 1) * MODES, :] = col
+            hi, lo = split(jnp.exp2(col * back), 2)
+            eb[g, k * MODES:(k + 1) * MODES, 0:LANES] = hi
+            eb[g, k * MODES:(k + 1) * MODES, LANES:2 * LANES] = lo
         lame[:, g * LANES:(g + 1) * LANES] = spread
-        rates = jnp.concatenate(cols, axis=0)
-        lamc[g * LANES:(g + 1) * LANES, :] = rates
-        weight = jnp.concatenate(rescols, axis=0) * jnp.sqrt(one_minus_exp_neg(2.0 * rates))
-        wc[g * LANES:(g + 1) * LANES, :] = weight
-        e = jnp.exp(-rates * back)
-        hi, lo = split(e, 2)
-        eb[g, 0:LANES, :] = hi
-        eb[g, LANES:2 * LANES, :] = lo
-        modal = jnp.where(lane128 == 0, weight, weight * e)
-        gh[g * 8:(g + 1) * 8, :] = jnp.sum(modal.reshape(8, MODES, LANES), axis=1)
 
     for c in range(chunks):
         rows = pl.ds(c * MED, MED)
-        pltpu.make_async_copy(k_hbm.at[rows], kbuf.at[rows], in_sem.at[0, c]).wait()
-        pltpu.make_async_copy(v_hbm.at[rows], vbuf.at[rows], in_sem.at[1, c]).wait()
-        xbuf[rows, :] = (kbuf[rows, :].astype(F32) * vbuf[rows, :].astype(F32)).astype(BF16)
-
-    own16 = iota((MODES, LANES), 1) // GW
+        for copy in fetch_rows(c):
+            copy.wait()
+        xbuf[rows, :] = kbuf[rows, :] * vbuf[rows, :]
+
     for g in range(tiles):
         lanes = slice(g * LANES, (g + 1) * LANES)
         total = None
-        d128 = jnp.exp(lame[:, lanes] * (-float(MED)))
-        both = [xbuf[c * MED:(c + 1) * MED, lanes] for c in range(chunks)]
-        raw = dot(eb[g], jnp.concatenate(both, axis=1))
-        raw = raw[0:LANES] + raw[LANES:2 * LANES]
+        d128 = jnp.exp2(lame[:, lanes] * (-float(MED)))
+        both = jnp.concatenate([xbuf[c * MED:(c + 1) * MED, lanes] for c in range(chunks)], axis=1)
+        raw = dot(eb[g], jnp.concatenate([both, both], axis=0))
         for c in range(chunks):
             part = jnp.zeros((MODES, LANES), F32)
             for k in range(8):
@@ -174,12 +182,13 @@
     def _():
         halo().start()
 
-    plan = plan_ref[...]
+    get_plan.wait()
+    plan = jnp.transpose(plan_v[...].astype(F32))
     tri = (iota((groups, groups), 1) < iota((groups, groups), 0)).astype(BF16)
 
     @pl.when(me == last)
     def _():
-        who = iota((groups, LANES), 1)
+        who = iota((groups, LANES), 1).astype(F32)
         hits = jnp.zeros((groups, LANES), F32)
         for b in range(NB + 1):
             hits = hits + (plan[:, b:b + 1] == who).astype(F32)
@@ -188,12 +197,10 @@
         for b in range(NB):
             reader = plan[:, b:b + 1]
             rank = jnp.sum(jnp.where(reader == who, before, 0.0), axis=1, keepdims=True)
-            slot = reader.astype(F32) * SLOTS + rank
-            slots = jnp.where(who == b, slot, slots)
+            slots = jnp.where(who == b, reader * SLOTS + rank, slots)
         slots_t = jnp.transpose(slots)
         for b in range(NB):
             for half in range(2):
-                first = tokens - MED + b * MODES + half * 8
                 for g in range(tiles):
                     tile = xbuf[tokens - MED + b * MODES:tokens - MED + (b + 1) * MODES,
                                 g * LANES:(g + 1) * LANES].astype(F32)[half * 8:half * 8 + 8]
@@ -203,8 +210,8 @@
             count = nz * SLOTS
             base = part * count
             acc = jnp.zeros((count, 2 * LANES), F32)
+            target = (iota((count, groups), 0) + base).astype(F32)
             for b in range(NB):
-                target = (iota((count, groups), 0) + base).astype(F32)
                 pick = (target == slots_t[b:b + 1, 0:groups]).astype(BF16)
                 acc = acc + dot(pick, items[b * groups:(b + 1) * groups, :].astype(BF16))
             packed = acc.astype(BF16).reshape(nz, SLOTS, 2 * LANES)
@@ -221,11 +228,23 @@
         for part in range(ny - 1):
             pack_copy(part).start()
 
-    perm = (iota((LANES, LANES), 0) == (LANES - iota((LANES, LANES), 1)) % LANES).astype(BF16)
-    flipped = dot(jnp.concatenate(split(taps_ref[...], 3), axis=0), perm)
+    get_res.wait()
+    get_taps.wait()
+    weight_t = res_v[...] * jnp.sqrt(one_minus_exp_neg(2.0 * lam_t))
+    perm = (iota((LANES, LANES), 0) == (LANES - lane128) % LANES).astype(BF16)
+    flipped = dot(jnp.concatenate(split(taps_v[...], 3), axis=0), perm)
     flipped = flipped[0:groups] + flipped[groups:2 * groups] + flipped[2 * groups:3 * groups]
     gt[...] = flipped
-    gh[...] = gh[...] + flipped
+    zero16 = iota((MODES, LANES), 1) == 0
+    for g in range(tiles):
+        sums = []
+        for k in range(8):
+            f = g * 8 + k
+            at = slice(k * MODES, (k + 1) * MODES)
+            w = jnp.broadcast_to(weight_t[:, f:f + 1], (MODES, LANES))
+            e = eb[g, at, 0:LANES].astype(F32) + eb[g, at, LANES:2 * LANES].astype(F32)
+            sums.append(jnp.sum(jnp.where(zero16, w, w * e), axis=0, keepdims=True))
+        gh[g * 8:(g + 1) * 8, :] = jnp.concatenate(sums, axis=0) + flipped[g * 8:(g + 1) * 8]
 
     def conv_tile(g, carry):
         lanes = pl.ds(pl.multiple_of(g * LANES, LANES), LANES)
@@ -241,24 +260,31 @@
             a = pltpu.roll(jnp.broadcast_to(full[k:k + 1], (LANES, LANES)), 0, 1, stride=1, stride_axis=0)
             b = pltpu.roll(jnp.broadcast_to(taps[k:k + 1], (LANES, LANES)), 0, 1, stride=1, stride_axis=0)
             cols = slice(k * LANES, (k + 1) * LANES)
-            tmat[g, 0:LANES, cols] = jnp.where(lower, a, 0.0).astype(BF16)
-            tmat[g, LANES:2 * LANES, cols] = jnp.where(lower, 0.0, b).astype(BF16)
+            hi, lo = split(jnp.where(lower, a, 0.0), 2)
+            tmat[g, 0:LANES, cols] = hi
+            tmat[g, 2 * LANES:3 * LANES, cols] = lo
+            hi, lo = split(jnp.where(lower, 0.0, b), 2)
+            tmat[g, LANES:2 * LANES, cols] = hi
+            tmat[g, 3 * LANES:4 * LANES, cols] = lo
             keep = (which == k).astype(BF16)
             rhs[cols, 0:LANES] = x0 * keep
             rhs[cols, LANES:2 * LANES] = x1 * keep
             rhs[cols, 2 * LANES:3 * LANES] = x2 * keep
-        out = dot(tmat[g], rhs[:, 0:2 * LANES])
+        out = dot(tmat[g, 0:2 * LANES, :], rhs[:, 0:2 * LANES])
+        out = out + dot(tmat[g, 2 * LANES:4 * LANES, :], rhs[:, 0:2 * LANES])
         out2 = dot(tmat[g, 0:LANES, :], rhs[:, 2 * LANES:3 * LANES])
+        out2 = out2 + dot(tmat[g, 2 * LANES:3 * LANES, :], rhs[:, 2 * LANES:3 * LANES])
         local[0:MED, lanes] = out[0:LANES, 0:LANES]
         local[MED:2 * MED, lanes] = out[0:LANES, LANES:2 * LANES] + out[LANES:2 * LANES, 0:LANES]
         local[2 * MED:3 * MED, lanes] = out2 + out[LANES:2 * LANES, LANES:2 * LANES]
         return carry
 
-    lax.fori_loop(0, tiles, conv_tile, 0)
+    early = 3 * tiles // 8
+    lax.fori_loop(0, early, conv_tile, 0)
 
     mine = pl.ds(pl.multiple_of(z * LANES, LANES), LANES)
     lam_s = lame[:, mine]
-    d_dev = jnp.exp(lam_s * (-float(tokens)))
+    d_dev = jnp.exp2(lam_s * (-float(tokens)))
     for d in range(1, nz):
         frm = (z - d + nz) % nz
         remote(a1s.at[0], a1r.at[frm], s1.at[d], r1.at[frm], me, ch).wait_recv()
@@ -276,13 +302,16 @@
         sent2.append(copy)
     a2r[y] = a2s[...]
 
-    def carry_tile(g, carry):
-        lanes = pl.ds(pl.multiple_of(g * LANES, LANES), LANES)
+    lax.fori_loop(early, tiles, conv_tile, 0)
+
+    for g in range(tiles):
+        lanes = slice(g * LANES, (g + 1) * LANES)
         rates = lamc[lanes, :]
-        weight = wc[lanes, :]
+        weight = jnp.concatenate(
+            [jnp.broadcast_to(weight_t[:, f:f + 1], (MODES, LANES)) for f in range(g * 8, g * 8 + 8)], axis=0)
         at = lane128.astype(F32)
         for c in range(chunks):
-            s = weight * jnp.exp(-rates * (at + float(c * MED)))
+            s = weight * jnp.exp2(-rates * (at + float(c * MED)))
             smat[c * MED:(c + 1) * MED, lanes] = jnp.transpose(s).astype(BF16)
         same = (iota((LANES, LANES), 0) // MODES) == (iota((LANES, LANES), 1) // GW)
         pieces = []
@@ -291,15 +320,12 @@
             pieces.append(jnp.where(same, state, 0.0))
         hi, lo = split(jnp.concatenate(pieces, axis=1), 2)
         factor = smat[0:MED, lanes]
-        out = dot(factor, hi) + dot(factor, lo)
+        out = dot(jnp.concatenate([factor, factor], axis=1), jnp.concatenate([hi, lo], axis=0))
         for c in range(chunks - 1):
             rows = slice((c + 1) * MED, (c + 2) * MED)
             local[rows, lanes] = local[rows, lanes] + out[:, c * LANES:(c + 1) * LANES]
-        return carry
-
-    lax.fori_loop(0, tiles, carry_tile, 0)
-
-    d_row = jnp.exp(lam_s * (-float(tokens * nz)))
+
+    d_row = jnp.exp2(lam_s * (-float(tokens * nz)))
     for d in range(1, ny):
         frm = (y - d + ny) % ny
         remote(a2s, a2r.at[frm], s2.at[d], r2.at[frm], me, ch).wait_recv()
@@ -308,7 +334,7 @@
     for i in range(ny):
         above = jnp.where(y == i, run, above)
         run = run * d_row + a2r[i].astype(F32)
-    norm_s = jnp.sqrt(one_minus_exp_neg(2.0 * lam_s))
+    norm_s = jnp.sqrt(one_minus_exp_neg(lam_s * (2.0 * LN2)))
     final = (run * norm_s).astype(BF16)
     for i in range(nz):
         a3s[i, 0] = (above + pre[i]).astype(BF16)
@@ -347,12 +373,13 @@
             for k in range(8):
                 rhs[k * LANES:(k + 1) * LANES, 0:LANES] = xh * (which == k).astype(BF16)
             out = dot(tmat[g, LANES:2 * LANES, :], rhs[:, 0:LANES])
+            out = out + dot(tmat[g, 3 * LANES:4 * LANES, :], rhs[:, 0:LANES])
             local[0:MED, lanes] = local[0:MED, lanes] + out
             return carry
 
         lax.fori_loop(0, tiles, halo_tile, 0)
 
-    pltpu.make_async_copy(q_hbm, qbuf, in_sem.at[2, 0]).wait()
+    get_q.wait()
     for d in range(1, nz):
         frm = (z - d + nz) % nz
         remote(a3s.at[0], a3r.at[frm], s3.at[d], r3.at[frm], me, ch).wait_recv()
@@ -379,11 +406,11 @@
         sentx.append(copy)
     er[ch] = es[...]
 
-    mine_hit = (plan == me)
-    hit = jnp.sum(mine_hit.astype(F32), axis=1, keepdims=True)
+    mine_hit = (plan == me.astype(F32)).astype(F32)
+    hit = jnp.sum(mine_hit, axis=1, keepdims=True)
     before = dot(tri, jnp.broadcast_to(hit, (groups, 2 * LANES)).astype(BF16))
     slot = (iota((groups, 2 * LANES), 1) // GW).astype(F32)
-    wants = ((before == slot) & mine_hit[:, NB:NB + 1]).astype(BF16)
+    wants = jnp.where(before == slot, mine_hit[:, NB:NB + 1], 0.0).astype(BF16)
     picked = jnp.zeros((MODES, 2 * LANES), F32)
     delta = ((iota((LANES, 2 * LANES), 0) % GW) == (iota((LANES, 2 * LANES), 1) % GW)).astype(F32)
     for g in range(tiles):
@@ -405,41 +432,53 @@
                 if j < 10:
                     hand_ref[j, 8 * b:8 * b + 8, :] = block[:, k * GW:(k + 1) * GW]
 
+    for copy in sent1 + sent2 + sent3:
+        copy.wait_send()
+
+    @pl.when(me < last)
+    def _():
+        halo().wait_send()
+
+    @pl.when(me == last)
+    def _():
+        for part in range(ny - 1):
+            pack_copy(part).wait_send()
+
+    @pl.when(z == nz - 1)
+    def _():
+        for to in range(nz - 1):
+            hop_copy(to).wait_send()
+
     for d in range(1, nc):
         frm = (ch - d + nc) % nc
         remote(es, er.at[frm], sx.at[d], rx.at[frm], me, ch).wait_recv()
     energy = er[0]
     for i in range(1, nc):
         energy = energy + er[i]
-    scale = lax.rsqrt(energy / (nc * tiles * LANES) + 1e-05)
+    energy_ref[...] = energy
+    for copy in sentx:
+        copy.wait_send()
+
+
+def finish(width, gated_ref, hand_ref, energy_ref, gain_ref, out_hbm, hand_hbm, obuf, sem):
+    tokens, channels = gated_ref.shape
+    chunks = tokens // MED
+    give = pltpu.make_async_copy(hand_ref, hand_hbm, sem.at[chunks])
+    give.start()
+    scale = lax.rsqrt(energy_ref[...] / width + 1e-05)
     scale = jnp.transpose(jnp.broadcast_to(scale, (LANES, tokens)))
+    copies = []
     for c in range(chunks):
         rows = slice(c * MED, (c + 1) * MED)
-        for g in range(tiles):
+        for g in range(channels // LANES):
             lanes = slice(g * LANES, (g + 1) * LANES)
-            obuf[rows, lanes] = (local[rows, lanes] * scale[rows] * gain_ref[:, lanes]).astype(BF16)
-        pltpu.make_async_copy(obuf.at[rows], out_hbm.at[rows], out_sem.at[c]).start()
-
-    for copy in sent1 + sent2 + sent3 + sentx:
-        copy.wait_send()
-
-    @pl.when(me < last)
-    def _():
-        halo().wait_send()
-
-    @pl.when(me == last)
-    def _():
-        for part in range(ny - 1):
-            pack_copy(part).wait_send()
-
-    @pl.when(z == nz - 1)
-    def _():
-        for to in range(nz - 1):
-            hop_copy(to).wait_send()
-
-    for c in range(chunks):
-        rows = slice(c * MED, (c + 1) * MED)
-        pltpu.make_async_copy(obuf.at[rows], out_hbm.at[rows], out_sem.at[c]).wait()
+            obuf[rows, lanes] = (gated_ref[rows, lanes] * scale[rows] * gain_ref[:, lanes]).astype(BF16)
+        copy = pltpu.make_async_copy(obuf.at[pl.ds(c * MED, MED)], out_hbm.at[pl.ds(c * MED, MED)], sem.at[c])
+        copy.start()
+        copies.append(copy)
+    for copy in copies:
+        copy.wait()
+    give.wait()
 
 
 def per_device(query_rows, key_rows, value_rows, residues, decay_rates, medium_taps, out_gain, reader_plan):
@@ -457,37 +496,50 @@
     scratch = [
         vm((tokens, channels), BF16), vm((tokens, channels), BF16), vm((tokens, channels), BF16),
         vm((tokens, channels), BF16), vm((MED, channels), BF16),
-        vm((channels, LANES), F32), vm((channels, LANES), F32), vm((tiles, 2 * LANES, LANES), BF16),
+        vm((MODES, groups), F32), vm((MODES, groups), F32), vm((groups, MED), F32), vm((NB + 1, groups), jnp.int32),
+        vm((channels, LANES), F32), vm((tiles, LANES, 2 * LANES), BF16),
         vm((MODES, channels), F32), vm((groups, LANES), F32), vm((groups, LANES), F32),
-        vm((tiles, 2 * LANES, 8 * LANES), BF16), vm((tokens, channels), BF16),
-        vm((8 * LANES, 3 * LANES), BF16), vm((tokens, channels), F32),
+        vm((tiles, 4 * LANES, 8 * LANES), BF16), vm((tokens, channels), BF16),
+        vm((8 * LANES, 3 * LANES), BF16),
         vm((chunks, MODES, channels), F32),
         vm((nz, MODES, LANES), BF16), vm((nz, MODES, LANES), BF16), vm((nz, MODES, LANES), F32),
         vm((MODES, LANES), BF16), vm((ny, MODES, LANES), BF16),
         vm((nz, 2, MODES, LANES), BF16), vm((nz, 2, MODES, LANES), BF16),
         vm((NB * groups, 2 * LANES), F32), vm((ny - 1, nz, SLOTS, 2 * LANES), BF16),
         vm((nz, SLOTS, 2 * LANES), BF16), vm((SLOTS, 2 * LANES), BF16),
-        vm((1, tokens), F32), vm((nc, 1, tokens), F32), vm((tokens, channels), BF16),
-        dma((3, chunks)), dma((chunks,)),
+        vm((1, tokens), F32), vm((nc, 1, tokens), F32),
+        dma((4, chunks)),
         dma((nz,)), dma((nz,)), dma((ny,)), dma((ny,)), dma((nz,)), dma((nz,)), dma((nc,)), dma((nc,)),
         dma, dma, dma((ny,)), dma, dma((nz,)), dma,
     ]
-    hbm = pl.BlockSpec(memory_space=pl.ANY)
+    hbm = pl.BlockSpec(memory_space=pltpu.HBM)
     vmem = pl.BlockSpec(memory_space=pltpu.VMEM)
-    return pl.pallas_call(
+    gated, hand, energy = pl.pallas_call(
         functools.partial(kernel, cfg),
         name="hyena",
+        out_shape=(
+            jax.ShapeDtypeStruct((tokens, channels), F32),
+            jax.ShapeDtypeStruct((10, MODES, GW), F32),
+            jax.ShapeDtypeStruct((1, tokens), F32),
+        ),
+        in_specs=[hbm] * 7,
+        out_specs=(vmem, vmem, vmem),
+        scratch_shapes=scratch,
+        compiler_params=pltpu.CompilerParams(
+            collective_id=0, has_side_effects=True, vmem_limit_bytes=48 * 1024 * 1024),
+    )(*[pltpu.with_memory_space_constraint(a, pltpu.HBM) for a in (query_rows, key_rows, value_rows, residues.T, decay_rates.T, medium_taps, reader_plan.T)])
+    return pl.pallas_call(
+        functools.partial(finish, nc * channels),
+        name="finish",
         out_shape=(
             jax.ShapeDtypeStruct((tokens, channels), BF16),
             jax.ShapeDtypeStruct((10, MODES, GW), F32),
         ),
-        in_specs=[hbm, hbm, hbm, vmem, vmem, vmem, vmem, vmem],
-        out_specs=(hbm, vmem),
-        scratch_shapes=scratch,
-        compiler_params=pltpu.CompilerParams(
-            collective_id=0, has_side_effects=True, vmem_limit_bytes=48 * 1024 * 1024),
-    )(query_rows, key_rows, value_rows, residues, decay_rates, medium_taps,
-      out_gain.reshape(1, channels), reader_plan)
+        in_specs=[vmem] * 4,
+        out_specs=(hbm, hbm),
+        scratch_shapes=[vm((tokens, channels), BF16), dma((chunks + 1,))],
+        compiler_params=pltpu.CompilerParams(vmem_limit_bytes=48 * 1024 * 1024),
+    )(gated, hand, energy, out_gain.reshape(1, channels))
 
 
 def solution(mesh):

time: 45.6 us -> 38.2 us (0.84)
  local copies, waits for them, and re-layouts: 7.08 us -> 0.01 us
    unnamed x19 -> x2, local copies, waits for them, and re-layouts: 7.08 us -> 0.01 us
    pallas_call x1, Pallas kernels: 37.4 us -> 36.3 us  [per_device(): pl.pallas_call(functools.partial(kernel, cfg), name='hyena', out_shape=(j...]
    pallas_call x0 -> x1, Pallas kernels: none -> 1.09 us  [per_device(): pl.pallas_call(functools.partial(finish, nc * channels), name='finish', o...]
where the time goes in v2:
time: 38.2 us; the launch traced here: 38 us
  Pallas kernels  37.3 us (98%)
  between operations  0.66 us (2%)
    pallas_call x1, Pallas kernels, per_device(): pl.pallas_call(functools.partial(kernel, cfg), name='hyena', out_shape=(j...  36.3 us
    pallas_call x1, Pallas kernels, per_device(): pl.pallas_call(functools.partial(finish, nc * channels), name='finish', o...  1.09 us

profile of v2, /device:TPU:1, one launch (start us, length us, event | category | flops | bytes accessed | tf_op | source)
XLA Modules:
  0.0 38.0 jit_solution(1221463696739414494)
XLA Ops:
  0.6 0.0 copy-start
  0.6 36.3 %hyena.1 = (f32[384,1024]{1,0:T(8,128)S(1)}, f32[10,16,16]{2,1,0:T(8,128)S(1)}, f32[1,384]{1,0:T(1,128)S(1)}) custom-call(bf16[384,1024]{1,0:T(8,128)(2,1)} %q_hbm.1, bf16[384,1024]{1,0:T(8,128)(2,1)} %k_hbm.1, bf16[384,1024]{1,0:T(8,128)(2,1)} %v_hbm.1, f32[16,64]{1,0:T(8,128)} %bitcast.5, f32[16,64]{1,0:T(8,128)} %bitcast.6, f32[64,128]{1,0:T(8,128)} %taps_hbm.1, ...), custom_call_target="tpu_custom_call" | custom-call | tf_op jit(solution)/shard_map/hyena/pallas_call | solution.py:517
  36.9 0.0 copy-done
  36.9 1.1 %finish.1 = (bf16[384,1024]{1,0:T(8,128)(2,1)}, f32[10,16,16]{2,1,0:T(8,128)}) custom-call(f32[384,1024]{1,0:T(8,128)S(1)} %get-tuple-element.5.gated_ref, f32[10,16,16]{2,1,0:T(8,128)S(1)} %get-tuple-element.6.hand_ref, f32[1,384]{1,0:T(1,128)S(1)} %get-tuple-element.7.energy_ref, f32[1,1024]{1,0:T(1,128)S(1)} %bitcast.4), custom_call_target="tpu_custom_call" | custom-call | tf_op jit(solution)/shard_map/finish/pallas_call | solution.py:531
Async XLA Ops:
  0.6 36.3 %copy-start = (f32[1024]{0:T(1024)S(1)}, f32[1024]{0:T(1024)}, u32[]{:S(2)}) copy-start(f32[1024]{0:T(1024)} %param.14) | copy-start | bytes 12292

commit v3 on v2

--- a/solution.py
+++ b/solution.py
@@ -129,9 +129,7 @@
             col = jnp.broadcast_to(lam2[:, f:f + 1], (MODES, LANES))
             spread = jnp.where(own16 == k, col, spread)
             lamc[f * MODES:(f + 1) * MODES, :] = col
-            hi, lo = split(jnp.exp2(col * back), 2)
-            eb[g, k * MODES:(k + 1) * MODES, 0:LANES] = hi
-            eb[g, k * MODES:(k + 1) * MODES, LANES:2 * LANES] = lo
+            eb[g, k * MODES:(k + 1) * MODES, :] = jnp.exp2(col * back).astype(BF16)
         lame[:, g * LANES:(g + 1) * LANES] = spread
 
     for c in range(chunks):
@@ -145,7 +143,7 @@
         total = None
         d128 = jnp.exp2(lame[:, lanes] * (-float(MED)))
         both = jnp.concatenate([xbuf[c * MED:(c + 1) * MED, lanes] for c in range(chunks)], axis=1)
-        raw = dot(eb[g], jnp.concatenate([both, both], axis=0))
+        raw = dot(eb[g], both)
         for c in range(chunks):
             part = jnp.zeros((MODES, LANES), F32)
             for k in range(8):
@@ -164,23 +162,20 @@
             src_ref=src, dst_ref=dst, send_sem=send, recv_sem=recv,
             device_id=(seq, chan), device_id_type=MESH)
 
+    def settle(ref, sem):
+        pltpu.make_async_copy(ref, ref, sem).wait()
+
     def order(n):
         return sorted(range(1, n), key=lambda d: -min(d, n - d))
 
-    sent1 = []
     for d in order(nz):
         to = (z + d) % nz
-        copy = remote(a1s.at[to], a1r.at[z], s1.at[d], r1.at[z], y * nz + to, ch)
+        copy = remote(a1s.at[to], a1r.at[z], s1, r1, y * nz + to, ch)
         copy.start()
-        sent1.append(copy)
     a1r[z] = a1s[z]
 
     def halo():
         return remote(xbuf.at[pl.ds(tokens - MED, MED)], hbuf, sh, rh, me + 1, ch)
-
-    @pl.when(me < last)
-    def _():
-        halo().start()
 
     get_plan.wait()
     plan = jnp.transpose(plan_v[...].astype(F32))
@@ -197,7 +192,9 @@
         for b in range(NB):
             reader = plan[:, b:b + 1]
             rank = jnp.sum(jnp.where(reader == who, before, 0.0), axis=1, keepdims=True)
-            slots = jnp.where(who == b, reader * SLOTS + rank, slots)
+            down = jnp.floor((reader + 0.5) * (1.0 / nz))
+            place = (reader - down * nz) * ny + down
+            slots = jnp.where(who == b, place * SLOTS + rank, slots)
         slots_t = jnp.transpose(slots)
         for b in range(NB):
             for half in range(2):
@@ -206,26 +203,28 @@
                                 g * LANES:(g + 1) * LANES].astype(F32)[half * 8:half * 8 + 8]
                     items[b * groups + g * 8:b * groups + g * 8 + 8,
                           half * LANES:(half + 1) * LANES] = swap_blocks(tile[None])[0]
-        for part in range(ny):
-            count = nz * SLOTS
+        wanted = [jnp.concatenate([slots_t[b:b + 1, 0:groups] for b in range(4 * i, 4 * i + 4)], axis=1)
+                  for i in range(NB // 4)]
+        for part in range(nz):
+            count = ny * SLOTS
             base = part * count
             acc = jnp.zeros((count, 2 * LANES), F32)
-            target = (iota((count, groups), 0) + base).astype(F32)
-            for b in range(NB):
-                pick = (target == slots_t[b:b + 1, 0:groups]).astype(BF16)
-                acc = acc + dot(pick, items[b * groups:(b + 1) * groups, :].astype(BF16))
-            packed = acc.astype(BF16).reshape(nz, SLOTS, 2 * LANES)
-            if part == ny - 1:
+            target = (iota((count, 4 * groups), 0) + base).astype(F32)
+            for b in range(NB // 4):
+                pick = (target == wanted[b]).astype(BF16)
+                acc = acc + dot(pick, items[4 * b * groups:4 * (b + 1) * groups, :].astype(BF16))
+            packed = acc.astype(BF16).reshape(ny, SLOTS, 2 * LANES)
+            if part == nz - 1:
                 row[...] = packed
             else:
                 pk[part] = packed
 
     def pack_copy(part):
-        return remote(pk.at[part], row, sp.at[part], rp, part * nz + nz - 1, ch)
+        return remote(pk.at[part], row, sp, rp, (ny - 1) * nz + part, ch)
 
     @pl.when(me == last)
     def _():
-        for part in range(ny - 1):
+        for part in range(nz - 1):
             pack_copy(part).start()
 
     get_res.wait()
@@ -240,13 +239,12 @@
         sums = []
         for k in range(8):
             f = g * 8 + k
-            at = slice(k * MODES, (k + 1) * MODES)
             w = jnp.broadcast_to(weight_t[:, f:f + 1], (MODES, LANES))
-            e = eb[g, at, 0:LANES].astype(F32) + eb[g, at, LANES:2 * LANES].astype(F32)
+            e = jnp.exp2(lamc[f * MODES:(f + 1) * MODES, :] * back)
             sums.append(jnp.sum(jnp.where(zero16, w, w * e), axis=0, keepdims=True))
         gh[g * 8:(g + 1) * 8, :] = jnp.concatenate(sums, axis=0) + flipped[g * 8:(g + 1) * 8]
 
-    def conv_tile(g, carry):
+    def conv_build(g, side):
         lanes = pl.ds(pl.multiple_of(g * LANES, LANES), LANES)
         rows8 = pl.ds(pl.multiple_of(g * 8, 8), 8)
         full = gh[rows8, :]
@@ -260,49 +258,53 @@
             a = pltpu.roll(jnp.broadcast_to(full[k:k + 1], (LANES, LANES)), 0, 1, stride=1, stride_axis=0)
             b = pltpu.roll(jnp.broadcast_to(taps[k:k + 1], (LANES, LANES)), 0, 1, stride=1, stride_axis=0)
             cols = slice(k * LANES, (k + 1) * LANES)
-            hi, lo = split(jnp.where(lower, a, 0.0), 2)
-            tmat[g, 0:LANES, cols] = hi
-            tmat[g, 2 * LANES:3 * LANES, cols] = lo
-            hi, lo = split(jnp.where(lower, 0.0, b), 2)
-            tmat[g, LANES:2 * LANES, cols] = hi
-            tmat[g, 3 * LANES:4 * LANES, cols] = lo
+            tmat[g, 0:LANES, cols] = jnp.where(lower, a, 0.0).astype(BF16)
+            tmat[g, LANES:2 * LANES, cols] = jnp.where(lower, 0.0, b).astype(BF16)
             keep = (which == k).astype(BF16)
-            rhs[cols, 0:LANES] = x0 * keep
-            rhs[cols, LANES:2 * LANES] = x1 * keep
-            rhs[cols, 2 * LANES:3 * LANES] = x2 * keep
-        out = dot(tmat[g, 0:2 * LANES, :], rhs[:, 0:2 * LANES])
-        out = out + dot(tmat[g, 2 * LANES:4 * LANES, :], rhs[:, 0:2 * LANES])
-        out2 = dot(tmat[g, 0:LANES, :], rhs[:, 2 * LANES:3 * LANES])
-        out2 = out2 + dot(tmat[g, 2 * LANES:3 * LANES, :], rhs[:, 2 * LANES:3 * LANES])
+            rhs[side, cols, 0:LANES] = x0 * keep
+            rhs[side, cols, LANES:2 * LANES] = x1 * keep
+            rhs[side, cols, 2 * LANES:3 * LANES] = x2 * keep
+
+    def conv_apply(g, side):
+        lanes = pl.ds(pl.multiple_of(g * LANES, LANES), LANES)
+        out = dot(tmat[g], rhs[side, :, 0:2 * LANES])
+        out2 = dot(tmat[g, 0:LANES, :], rhs[side, :, 2 * LANES:3 * LANES])
         local[0:MED, lanes] = out[0:LANES, 0:LANES]
         local[MED:2 * MED, lanes] = out[0:LANES, LANES:2 * LANES] + out[LANES:2 * LANES, 0:LANES]
         local[2 * MED:3 * MED, lanes] = out2 + out[LANES:2 * LANES, LANES:2 * LANES]
+
+    def conv_pair(p, carry):
+        conv_build(2 * p, 0)
+        conv_build(2 * p + 1, 1)
+        conv_apply(2 * p, 0)
+        conv_apply(2 * p + 1, 1)
         return carry
 
-    early = 3 * tiles // 8
-    lax.fori_loop(0, early, conv_tile, 0)
+    pairs = tiles // 2
+    early = jnp.where(me == last, pairs // 4, 3 * pairs // 4)
+    lax.fori_loop(0, early, conv_pair, 0)
 
     mine = pl.ds(pl.multiple_of(z * LANES, LANES), LANES)
     lam_s = lame[:, mine]
     d_dev = jnp.exp2(lam_s * (-float(tokens)))
-    for d in range(1, nz):
-        frm = (z - d + nz) % nz
-        remote(a1s.at[0], a1r.at[frm], s1.at[d], r1.at[frm], me, ch).wait_recv()
+    settle(a1r.at[pl.ds(0, nz - 1)], r1)
     run = jnp.zeros((MODES, LANES), F32)
     for i in range(nz):
         pre[i] = run
         run = run * d_dev + a1r[i].astype(F32)
     a2s[...] = run.astype(BF16)
 
-    sent2 = []
     for d in order(ny):
         to = (y + d) % ny
-        copy = remote(a2s, a2r.at[y], s2.at[d], r2.at[y], to * nz + z, ch)
+        copy = remote(a2s, a2r.at[y], s2, r2, to * nz + z, ch)
         copy.start()
-        sent2.append(copy)
     a2r[y] = a2s[...]
 
-    lax.fori_loop(early, tiles, conv_tile, 0)
+    @pl.when(me < last)
+    def _():
+        halo().start()
+
+    lax.fori_loop(early, pairs, conv_pair, 0)
 
     for g in range(tiles):
         lanes = slice(g * LANES, (g + 1) * LANES)
@@ -326,9 +328,7 @@
             local[rows, lanes] = local[rows, lanes] + out[:, c * LANES:(c + 1) * LANES]
 
     d_row = jnp.exp2(lam_s * (-float(tokens * nz)))
-    for d in range(1, ny):
-        frm = (y - d + ny) % ny
-        remote(a2s, a2r.at[frm], s2.at[d], r2.at[frm], me, ch).wait_recv()
+    settle(a2r.at[pl.ds(0, ny - 1)], r2)
     run = jnp.zeros((MODES, LANES), F32)
     above = jnp.zeros((MODES, LANES), F32)
     for i in range(ny):
@@ -341,26 +341,24 @@
         a3s[i, 1] = final
         above = above * d_dev
 
-    sent3 = []
     for d in order(nz):
         to = (z + d) % nz
-        copy = remote(a3s.at[to], a3r.at[z], s3.at[d], r3.at[z], y * nz + to, ch)
+        copy = remote(a3s.at[to], a3r.at[z], s3, r3, y * nz + to, ch)
         copy.start()
-        sent3.append(copy)
     a3r[z] = a3s[z]
 
     def hop_copy(to):
-        return remote(row.at[to], tin, sf.at[to], rf, y * nz + to, ch)
-
-    @pl.when((z == nz - 1) & (me != last))
-    def _():
-        remote(pk.at[0], row, sp.at[0], rp, me, ch).wait_recv()
-
-    @pl.when(z == nz - 1)
-    def _():
-        for to in range(nz - 1):
+        return remote(row.at[to], tin, sf, rf, to * nz + z, ch)
+
+    @pl.when((y == ny - 1) & (me != last))
+    def _():
+        remote(pk.at[0], row, sp, rp, me, ch).wait_recv()
+
+    @pl.when(y == ny - 1)
+    def _():
+        for to in range(ny - 1):
             hop_copy(to).start()
-        tin[...] = row[nz - 1]
+        tin[...] = row[ny - 1]
 
     @pl.when(me > 0)
     def _():
@@ -371,18 +369,15 @@
             which = iota((MED, LANES), 1) // GW
             xh = hbuf[:, lanes]
             for k in range(8):
-                rhs[k * LANES:(k + 1) * LANES, 0:LANES] = xh * (which == k).astype(BF16)
-            out = dot(tmat[g, LANES:2 * LANES, :], rhs[:, 0:LANES])
-            out = out + dot(tmat[g, 3 * LANES:4 * LANES, :], rhs[:, 0:LANES])
+                rhs[0, k * LANES:(k + 1) * LANES, 0:LANES] = xh * (which == k).astype(BF16)
+            out = dot(tmat[g, LANES:2 * LANES, :], rhs[0, :, 0:LANES])
             local[0:MED, lanes] = local[0:MED, lanes] + out
             return carry
 
         lax.fori_loop(0, tiles, halo_tile, 0)
 
     get_q.wait()
-    for d in range(1, nz):
-        frm = (z - d + nz) % nz
-        remote(a3s.at[0], a3r.at[frm], s3.at[d], r3.at[frm], me, ch).wait_recv()
+    settle(a3r.at[pl.ds(0, nz - 1)], r3)
 
     power = jnp.zeros((tokens, LANES), F32)
     wide = 2 * LANES
@@ -398,12 +393,10 @@
         power = power + sq[:, 0:LANES] + sq[:, LANES:wide]
     es[...] = jnp.sum(jnp.transpose(power), axis=0, keepdims=True)
 
-    sentx = []
     for d in order(nc):
         to = (ch + d) % nc
-        copy = remote(es, er.at[ch], sx.at[d], rx.at[ch], me, to)
+        copy = remote(es, er.at[ch], sx, rx, me, to)
         copy.start()
-        sentx.append(copy)
     er[ch] = es[...]
 
     mine_hit = (plan == me.astype(F32)).astype(F32)
@@ -418,9 +411,9 @@
         choose = (dot(rep, wants) * delta).astype(BF16)
         picked = picked + dot(a3r[g, 1], choose)
 
-    @pl.when(z != nz - 1)
-    def _():
-        remote(row.at[0], tin, sf.at[0], rf, me, ch).wait_recv()
+    @pl.when(y != ny - 1)
+    def _():
+        remote(row.at[0], tin, sf, rf, me, ch).wait_recv()
 
     tails = tin[...].astype(F32)
     for a in range(2):
@@ -432,8 +425,9 @@
                 if j < 10:
                     hand_ref[j, 8 * b:8 * b + 8, :] = block[:, k * GW:(k + 1) * GW]
 
-    for copy in sent1 + sent2 + sent3:
-        copy.wait_send()
+    settle(a1s.at[pl.ds(0, nz - 1)], s1)
+    settle(a2r.at[pl.ds(0, ny - 1)], s2)
+    settle(a3s.at[pl.ds(0, nz - 1)], s3)
 
     @pl.when(me < last)
     def _():
@@ -441,23 +435,18 @@
 
     @pl.when(me == last)
     def _():
-        for part in range(ny - 1):
-            pack_copy(part).wait_send()
-
-    @pl.when(z == nz - 1)
-    def _():
-        for to in range(nz - 1):
-            hop_copy(to).wait_send()
-
-    for d in range(1, nc):
-        frm = (ch - d + nc) % nc
-        remote(es, er.at[frm], sx.at[d], rx.at[frm], me, ch).wait_recv()
+        settle(pk, sp)
+
+    @pl.when(y == ny - 1)
+    def _():
+        settle(row.at[pl.ds(0, ny - 1)], sf)
+
+    settle(er.at[pl.ds(0, nc - 1)], rx)
     energy = er[0]
     for i in range(1, nc):
         energy = energy + er[i]
     energy_ref[...] = energy
-    for copy in sentx:
-        copy.wait_send()
+    settle(er.at[pl.ds(0, nc - 1)], sx)
 
 
 def finish(width, gated_ref, hand_ref, energy_ref, gain_ref, out_hbm, hand_hbm, obuf, sem):
@@ -497,20 +486,19 @@
         vm((tokens, channels), BF16), vm((tokens, channels), BF16), vm((tokens, channels), BF16),
         vm((tokens, channels), BF16), vm((MED, channels), BF16),
         vm((MODES, groups), F32), vm((MODES, groups), F32), vm((groups, MED), F32), vm((NB + 1, groups), jnp.int32),
-        vm((channels, LANES), F32), vm((tiles, LANES, 2 * LANES), BF16),
+        vm((channels, LANES), F32), vm((tiles, LANES, LANES), BF16),
         vm((MODES, channels), F32), vm((groups, LANES), F32), vm((groups, LANES), F32),
-        vm((tiles, 4 * LANES, 8 * LANES), BF16), vm((tokens, channels), BF16),
-        vm((8 * LANES, 3 * LANES), BF16),
+        vm((tiles, 2 * LANES, 8 * LANES), BF16), vm((tokens, channels), BF16),
+        vm((2, 8 * LANES, 3 * LANES), BF16),
         vm((chunks, MODES, channels), F32),
         vm((nz, MODES, LANES), BF16), vm((nz, MODES, LANES), BF16), vm((nz, MODES, LANES), F32),
         vm((MODES, LANES), BF16), vm((ny, MODES, LANES), BF16),
         vm((nz, 2, MODES, LANES), BF16), vm((nz, 2, MODES, LANES), BF16),
-        vm((NB * groups, 2 * LANES), F32), vm((ny - 1, nz, SLOTS, 2 * LANES), BF16),
-        vm((nz, SLOTS, 2 * LANES), BF16), vm((SLOTS, 2 * LANES), BF16),
+        vm((NB * groups, 2 * LANES), F32), vm((nz - 1, ny, SLOTS, 2 * LANES), BF16),
+        vm((ny, SLOTS, 2 * LANES), BF16), vm((SLOTS, 2 * LANES), BF16),
         vm((1, tokens), F32), vm((nc, 1, tokens), F32),
         dma((4, chunks)),
-        dma((nz,)), dma((nz,)), dma((ny,)), dma((ny,)), dma((nz,)), dma((nz,)), dma((nc,)), dma((nc,)),
-        dma, dma, dma((ny,)), dma, dma((nz,)), dma,
+        dma, dma, dma, dma, dma, dma, dma, dma, dma, dma, dma, dma, dma, dma,
     ]
     hbm = pl.BlockSpec(memory_space=pltpu.HBM)
     vmem = pl.BlockSpec(memory_space=pltpu.VMEM)

time: 38.2 us -> 35.9 us (0.940)
  Pallas kernels: 37.3 us -> 34.8 us
    pallas_call x1, Pallas kernels: 36.3 us -> 33.7 us  [per_device(): pl.pallas_call(functools.partial(kernel, cfg), name='hyena', out_shape=(j...]
where the time goes in v3:
time: 35.9 us; the launch traced here: 35.5 us
  Pallas kernels  34.8 us (97%)
  between operations  0.66 us (2%)
    pallas_call x1, Pallas kernels, per_device(): pl.pallas_call(functools.partial(kernel, cfg), name='hyena', out_shape=(j...  33.7 us
    pallas_call x1, Pallas kernels, per_device(): pl.pallas_call(functools.partial(finish, nc * channels), name='finish', o...  1.09 us

profile of v3, /device:TPU:1, one launch (start us, length us, event | category | flops | bytes accessed | tf_op | source)
XLA Modules:
  0.0 35.5 jit_solution(12779835593446583142)
XLA Ops:
  0.6 0.0 copy-start
  0.6 33.7 %hyena.1 = (f32[384,1024]{1,0:T(8,128)S(1)}, f32[10,16,16]{2,1,0:T(8,128)S(1)}, f32[1,384]{1,0:T(1,128)S(1)}) custom-call(bf16[384,1024]{1,0:T(8,128)(2,1)} %q_hbm.1, bf16[384,1024]{1,0:T(8,128)(2,1)} %k_hbm.1, bf16[384,1024]{1,0:T(8,128)(2,1)} %v_hbm.1, f32[16,64]{1,0:T(8,128)} %bitcast.5, f32[16,64]{1,0:T(8,128)} %bitcast.6, f32[64,128]{1,0:T(8,128)} %taps_hbm.1, ...), custom_call_target="tpu_custom_call" | custom-call | tf_op jit(solution)/shard_map/hyena/pallas_call | solution.py:505
  34.4 0.0 copy-done
  34.4 1.1 %finish.1 = (bf16[384,1024]{1,0:T(8,128)(2,1)}, f32[10,16,16]{2,1,0:T(8,128)}) custom-call(f32[384,1024]{1,0:T(8,128)S(1)} %get-tuple-element.5.gated_ref, f32[10,16,16]{2,1,0:T(8,128)S(1)} %get-tuple-element.6.hand_ref, f32[1,384]{1,0:T(1,128)S(1)} %get-tuple-element.7.energy_ref, f32[1,1024]{1,0:T(1,128)S(1)} %bitcast.4), custom_call_target="tpu_custom_call" | custom-call | tf_op jit(solution)/shard_map/finish/pallas_call | solution.py:519
Async XLA Ops:
  0.6 33.7 %copy-start = (f32[1024]{0:T(1024)S(1)}, f32[1024]{0:T(1024)}, u32[]{:S(2)}) copy-start(f32[1024]{0:T(1024)} %param.14) | copy-start | bytes 12292

commit v4 on v3

--- a/solution.py
+++ b/solution.py
@@ -14,6 +14,7 @@
 MED = 128
 NB = 8
 SLOTS = 16
+PIECE = 64
 LANES = 128
 F32 = jnp.float32
 BF16 = jnp.bfloat16
@@ -59,9 +60,9 @@
     return out
 
 
-def kernel(cfg, q_hbm, k_hbm, v_hbm, res_hbm, lam_hbm, taps_hbm, plan_hbm,
+def kernel(cfg, q_hbm, k_hbm, v_hbm, res_hbm, lam_hbm, taps_hbm, plan_hbm, gain_hbm,
            local, hand_ref, energy_ref,
-           kbuf, vbuf, qbuf, xbuf, hbuf, lam_v, res_v, taps_v, plan_v, lamc, eb, lame, gh, gt, tmat, smat, rhs, st,
+           kbuf, vbuf, qbuf, xbuf, hbuf, lam_v, res_v, taps_v, plan_v, gain_v, lamc, eb, lame, gh, gt, tmat, smat, rhs, st,
            a1s, a1r, pre, a2s, a2r, a3s, a3r, items, pk, row, tin, es, er,
            in_sem, s1, r1, s2, r2, s3, r3, sx, rx, sh, rh, sp, rp, sf, rf):
     ny, nz, nc, tiles, tokens = cfg
@@ -73,6 +74,31 @@
     z = me % nz
     last = ny * nz - 1
 
+    def order(n):
+        return sorted(range(1, n), key=lambda d: -min(d, n - d))
+
+    barrier = pltpu.get_barrier_semaphore()
+
+    def greet(seq, chan):
+        pl.semaphore_signal(barrier, inc=1, device_id=(seq, chan), device_id_type=MESH)
+
+    for d in order(nz):
+        greet(y * nz + (z + d) % nz, ch)
+    for d in order(ny):
+        greet(((y + d) % ny) * nz + z, ch)
+    for d in order(nc):
+        greet(me, (ch + d) % nc)
+    wraps_on = (z == nz - 1) & (y < ny - 1)
+    wraps_in = (z == 0) & (y > 0)
+
+    @pl.when(wraps_on)
+    def _():
+        greet(me + 1, ch)
+
+    @pl.when(wraps_in)
+    def _():
+        greet(me - 1, ch)
+
     def fetch(src, dst, a, b):
         return pltpu.make_async_copy(src, dst, in_sem.at[a, b])
 
@@ -85,6 +111,7 @@
     get_taps = fetch(taps_hbm, taps_v, 2, 2)
     get_plan = fetch(plan_hbm, plan_v, 3, 0)
     get_q = fetch(q_hbm, qbuf, 3, 1)
+    get_gain = fetch(gain_hbm, gain_v, 3, 2)
     get_lam.start()
     for c in range(chunks):
         for copy in fetch_rows(c):
@@ -93,28 +120,7 @@
     get_taps.start()
     get_plan.start()
     get_q.start()
-
-    barrier = pltpu.get_barrier_semaphore()
-
-    def greet(seq, chan):
-        pl.semaphore_signal(barrier, inc=1, device_id=(seq, chan), device_id_type=MESH)
-
-    for d in range(1, nz):
-        greet(y * nz + (z + d) % nz, ch)
-    for d in range(1, ny):
-        greet(((y + d) % ny) * nz + z, ch)
-    for d in range(1, nc):
-        greet(me, (ch + d) % nc)
-    wraps_on = (z == nz - 1) & (y < ny - 1)
-    wraps_in = (z == 0) & (y > 0)
-
-    @pl.when(wraps_on)
-    def _():
-        greet(me + 1, ch)
-
-    @pl.when(wraps_in)
-    def _():
-        greet(me - 1, ch)
+    get_gain.start()
 
     get_lam.wait()
     lam_t = lam_v[...]
@@ -164,9 +170,6 @@
 
     def settle(ref, sem):
         pltpu.make_async_copy(ref, ref, sem).wait()
-
-    def order(n):
-        return sorted(range(1, n), key=lambda d: -min(d, n - d))
 
     for d in order(nz):
         to = (z + d) % nz
@@ -377,6 +380,7 @@
         lax.fori_loop(0, tiles, halo_tile, 0)
 
     get_q.wait()
+    get_gain.wait()
     settle(a3r.at[pl.ds(0, nz - 1)], r3)
 
     power = jnp.zeros((tokens, LANES), F32)
@@ -441,6 +445,10 @@
     def _():
         settle(row.at[pl.ds(0, ny - 1)], sf)
 
+    for g in range(tiles):
+        lanes = slice(g * LANES, (g + 1) * LANES)
+        local[:, lanes] = local[:, lanes] * gain_v[:, lanes]
+
     settle(er.at[pl.ds(0, nc - 1)], rx)
     energy = er[0]
     for i in range(1, nc):
@@ -449,20 +457,20 @@
     settle(er.at[pl.ds(0, nc - 1)], sx)
 
 
-def finish(width, gated_ref, hand_ref, energy_ref, gain_ref, out_hbm, hand_hbm, obuf, sem):
+def finish(width, gated_ref, hand_ref, energy_ref, out_hbm, hand_hbm, obuf, sem):
     tokens, channels = gated_ref.shape
-    chunks = tokens // MED
+    chunks = tokens // PIECE
     give = pltpu.make_async_copy(hand_ref, hand_hbm, sem.at[chunks])
     give.start()
     scale = lax.rsqrt(energy_ref[...] / width + 1e-05)
     scale = jnp.transpose(jnp.broadcast_to(scale, (LANES, tokens)))
     copies = []
     for c in range(chunks):
-        rows = slice(c * MED, (c + 1) * MED)
+        rows = slice(c * PIECE, (c + 1) * PIECE)
         for g in range(channels // LANES):
             lanes = slice(g * LANES, (g + 1) * LANES)
-            obuf[rows, lanes] = (gated_ref[rows, lanes] * scale[rows] * gain_ref[:, lanes]).astype(BF16)
-        copy = pltpu.make_async_copy(obuf.at[pl.ds(c * MED, MED)], out_hbm.at[pl.ds(c * MED, MED)], sem.at[c])
+            obuf[rows, lanes] = (gated_ref[rows, lanes] * scale[rows]).astype(BF16)
+        copy = pltpu.make_async_copy(obuf.at[pl.ds(c * PIECE, PIECE)], out_hbm.at[pl.ds(c * PIECE, PIECE)], sem.at[c])
         copy.start()
         copies.append(copy)
     for copy in copies:
@@ -485,7 +493,7 @@
     scratch = [
         vm((tokens, channels), BF16), vm((tokens, channels), BF16), vm((tokens, channels), BF16),
         vm((tokens, channels), BF16), vm((MED, channels), BF16),
-        vm((MODES, groups), F32), vm((MODES, groups), F32), vm((groups, MED), F32), vm((NB + 1, groups), jnp.int32),
+        vm((MODES, groups), F32), vm((MODES, groups), F32), vm((groups, MED), F32), vm((NB + 1, groups), jnp.int32), vm((1, channels), F32),
         vm((channels, LANES), F32), vm((tiles, LANES, LANES), BF16),
         vm((MODES, channels), F32), vm((groups, LANES), F32), vm((groups, LANES), F32),
         vm((tiles, 2 * LANES, 8 * LANES), BF16), vm((tokens, channels), BF16),
@@ -510,12 +518,12 @@
             jax.ShapeDtypeStruct((10, MODES, GW), F32),
             jax.ShapeDtypeStruct((1, tokens), F32),
         ),
-        in_specs=[hbm] * 7,
+        in_specs=[hbm] * 8,
         out_specs=(vmem, vmem, vmem),
         scratch_shapes=scratch,
         compiler_params=pltpu.CompilerParams(
             collective_id=0, has_side_effects=True, vmem_limit_bytes=48 * 1024 * 1024),
-    )(*[pltpu.with_memory_space_constraint(a, pltpu.HBM) for a in (query_rows, key_rows, value_rows, residues.T, decay_rates.T, medium_taps, reader_plan.T)])
+    )(*[pltpu.with_memory_space_constraint(a, pltpu.HBM) for a in (query_rows, key_rows, value_rows, residues.T, decay_rates.T, medium_taps, reader_plan.T, out_gain.reshape(1, channels))])
     return pl.pallas_call(
         functools.partial(finish, nc * channels),
         name="finish",
@@ -523,11 +531,11 @@
             jax.ShapeDtypeStruct((tokens, channels), BF16),
             jax.ShapeDtypeStruct((10, MODES, GW), F32),
         ),
-        in_specs=[vmem] * 4,
+        in_specs=[vmem] * 3,
         out_specs=(hbm, hbm),
-        scratch_shapes=[vm((tokens, channels), BF16), dma((chunks + 1,))],
+        scratch_shapes=[vm((tokens, channels), BF16), dma((tokens // PIECE + 1,))],
         compiler_params=pltpu.CompilerParams(vmem_limit_bytes=48 * 1024 * 1024),
-    )(gated, hand, energy, out_gain.reshape(1, channels))
+    )(gated, hand, energy)
 
 
 def solution(mesh):

time: 35.9 us -> 35.5 us (0.989)
  no operation moved by 1% of the time
where the time goes in v4:
time: 35.5 us; the launch traced here: 35.3 us
  Pallas kernels  34.7 us (98%)
  between operations  0.64 us (2%)
    pallas_call x1, Pallas kernels, per_device(): pl.pallas_call(functools.partial(kernel, cfg), name='hyena', out_shape=(j...  33.6 us
    pallas_call x1, Pallas kernels, per_device(): pl.pallas_call(functools.partial(finish, nc * channels), name='finish', o...  1.04 us

profile of v4, /device:TPU:1, one launch (start us, length us, event | category | flops | bytes accessed | tf_op | source)
XLA Modules:
  0.0 35.3 jit_solution(13588845595369410748)
XLA Ops:
  0.6 33.6 %hyena.1 = (f32[384,1024]{1,0:T(8,128)S(1)}, f32[10,16,16]{2,1,0:T(8,128)S(1)}, f32[1,384]{1,0:T(1,128)S(1)}) custom-call(bf16[384,1024]{1,0:T(8,128)(2,1)} %q_hbm.1, bf16[384,1024]{1,0:T(8,128)(2,1)} %k_hbm.1, bf16[384,1024]{1,0:T(8,128)(2,1)} %v_hbm.1, f32[16,64]{1,0:T(8,128)} %bitcast.4, f32[16,64]{1,0:T(8,128)} %bitcast.5, f32[64,128]{1,0:T(8,128)} %taps_hbm.1, ...), custom_call_target="tpu_custom_call" | custom-call | tf_op jit(solution)/shard_map/hyena/pallas_call | solution.py:513
  34.3 1.0 %finish.1 = (bf16[384,1024]{1,0:T(8,128)(2,1)}, f32[10,16,16]{2,1,0:T(8,128)}) custom-call(f32[384,1024]{1,0:T(8,128)S(1)} %get-tuple-element.5.gated_ref, f32[10,16,16]{2,1,0:T(8,128)S(1)} %get-tuple-element.6.hand_ref, f32[1,384]{1,0:T(1,128)S(1)} %get-tuple-element.7.energy_ref), custom_call_target="tpu_custom_call" | custom-call | tf_op jit(solution)/shard_map/finish/pallas_call | solution.py:527

commit v5 on v4

--- a/solution.py
+++ b/solution.py
@@ -284,7 +284,7 @@
         return carry
 
     pairs = tiles // 2
-    early = jnp.where(me == last, pairs // 4, 3 * pairs // 4)
+    early = jnp.where(me == last, pairs // 4, pairs // 2)
     lax.fori_loop(0, early, conv_pair, 0)
 
     mine = pl.ds(pl.multiple_of(z * LANES, LANES), LANES)

time: 35.5 us -> 35.4 us (level)
  no operation moved by 1% of the time
where the time goes in v5:
time: 35.4 us; the launch traced here: 35.3 us
  Pallas kernels  34.6 us (98%)
  between operations  0.64 us (2%)
    pallas_call x1, Pallas kernels, per_device(): pl.pallas_call(functools.partial(kernel, cfg), name='hyena', out_shape=(j...  33.6 us
    pallas_call x1, Pallas kernels, per_device(): pl.pallas_call(functools.partial(finish, nc * channels), name='finish', o...  1.04 us

profile of v5, /device:TPU:1, one launch (start us, length us, event | category | flops | bytes accessed | tf_op | source)
XLA Modules:
  0.0 35.3 jit_solution(5168560875725144456)
XLA Ops:
  0.6 33.6 %hyena.1 = (f32[384,1024]{1,0:T(8,128)S(1)}, f32[10,16,16]{2,1,0:T(8,128)S(1)}, f32[1,384]{1,0:T(1,128)S(1)}) custom-call(bf16[384,1024]{1,0:T(8,128)(2,1)} %q_hbm.1, bf16[384,1024]{1,0:T(8,128)(2,1)} %k_hbm.1, bf16[384,1024]{1,0:T(8,128)(2,1)} %v_hbm.1, f32[16,64]{1,0:T(8,128)} %bitcast.4, f32[16,64]{1,0:T(8,128)} %bitcast.5, f32[64,128]{1,0:T(8,128)} %taps_hbm.1, ...), custom_call_target="tpu_custom_call" | custom-call | tf_op jit(solution)/shard_map/hyena/pallas_call | solution.py:513
  34.2 1.0 %finish.1 = (bf16[384,1024]{1,0:T(8,128)(2,1)}, f32[10,16,16]{2,1,0:T(8,128)}) custom-call(f32[384,1024]{1,0:T(8,128)S(1)} %get-tuple-element.5.gated_ref, f32[10,16,16]{2,1,0:T(8,128)S(1)} %get-tuple-element.6.hand_ref, f32[1,384]{1,0:T(1,128)S(1)} %get-tuple-element.7.energy_ref), custom_call_target="tpu_custom_call" | custom-call | tf_op jit(solution)/shard_map/finish/pallas_call | solution.py:527
